TPU v7x, 256 devices: a whole 4x4x8 slice. The times are simulated.
256 devices in a mesh: req: 32 (over x, z), tp: 8 (over y, core).
Axes of the slice: x: 4, y: 4, z: 8, core: 2. Of those that a mesh axis runs over, the one named last changes fastest.
Arguments:
- inputs: bfloat16 [128, 1280], P('req'), may hold values from -6 to 6
- gain_attn: float32 [1280], replicated, may hold values from 0.25 to 1.75
- w_qkv: bfloat16 [3, 1280, 1280], P(None, 'tp'), may hold values from -0.15625 to 0.15625
- k_cache: bfloat16 [128, 1280, 2048], P('req', 'tp'), may hold values from -800 to 800
- v_cache: bfloat16 [128, 1280, 2048], P('req', 'tp'), may hold values from -6 to 6
- lengths: int32 [128], P('req'), may hold values from 128 to 2048, as said below
- pad_mask: int32 [128, 2048], P('req'), may hold values 0 or 1
- w_out: bfloat16 [1280, 1280], P('tp'), may hold values from -0.15625 to 0.15625
- gain_mlp: float32 [1280], replicated, may hold values from 0.25 to 1.75
- w_up: bfloat16 [1280, 1280], P('tp'), may hold values from -0.15625 to 0.15625
- w_down: bfloat16 [1280, 1280], P('tp'), may hold values from -0.15625 to 0.15625
- w_head: bfloat16 [1280, 1280], P('tp'), may hold values from -0.15625 to 0.15625
- placement: int32 [2, 64], replicated, may hold values from 0 to 63, as said below
- guide: float32 [64], P('req'), may hold values from 1.5 to 6
Outputs:
- guided: float32 [64, 1280], P('req', 'tp')
Inputs may be any that keep to these rules, and one draw needn't show every extreme that they name: `lengths`: some request has exactly 2048 filled slots. `placement`: each of the two rows is a permutation of 0 to 63.
All inputs are finite; a program needn't handle non-finite values. No bound on the sum of `pad_mask` on one device may be relied on, other than what follows from the above.
Results may differ from a plain program's by a relative error of at most 0.0085.
Values may be sent and summed in bfloat16 or wider, within the bound.
No kernel may reach another device: no remote copies, remote signals or barrier semaphores. Data moves between devices by JAX's collectives and lax.ppermute only.
A program may use at most 64 MiB of HBM per device.

v0:
```python
import jax
import jax.numpy as jnp
from jax import lax
from jax.sharding import PartitionSpec as P

HEAD_DIM = 80


def rms_gain(values, gain):
    return values * lax.rsqrt(jnp.mean(values * values, axis=-1, keepdims=True) + 1e-06) * gain


def project_rows(left, weight):
    return lax.dot_general(
        left, weight, (((1,), (1,)), ((), ())), preferred_element_type=jnp.float32
    )


def on_device(
    inputs,
    gain_attn,
    w_qkv,
    k_cache,
    v_cache,
    lengths,
    pad_mask,
    w_out,
    gain_mlp,
    w_up,
    w_down,
    w_head,
    placement,
    guide,
):
    rows = inputs.shape[0]
    local_width = w_qkv.shape[1]
    heads_here = local_width // HEAD_DIM
    scale = HEAD_DIM ** (-0.5)
    xvals = inputs.astype(jnp.float32)
    normed = rms_gain(xvals, gain_attn).astype(jnp.bfloat16)
    query = project_rows(normed, w_qkv[0]).astype(jnp.bfloat16).reshape(rows, heads_here, HEAD_DIM)
    key_new = (
        project_rows(normed, w_qkv[1]).astype(jnp.bfloat16).reshape(rows, heads_here, HEAD_DIM)
    )
    value_new = (
        project_rows(normed, w_qkv[2]).astype(jnp.bfloat16).reshape(rows, heads_here, HEAD_DIM)
    )
    own = jnp.sum(query.astype(jnp.float32) * key_new.astype(jnp.float32), axis=-1) * scale
    ctx_slots = k_cache.shape[2]
    block = min(512, ctx_slots)
    offsets = jnp.arange(block, dtype=jnp.int32)
    count = ctx_slots // block

    def score_pass(step, buffer):
        start = step * block
        kblock = lax.dynamic_slice_in_dim(k_cache, start, block, 2).reshape(
            rows, heads_here, HEAD_DIM, block
        )
        scores = (
            jnp.einsum("rhd,rhdb->rhb", query, kblock, preferred_element_type=jnp.float32) * scale
        )
        padrow = lax.dynamic_slice_in_dim(pad_mask, start, block, 1)
        valid = ((start + offsets)[None, :] < lengths[:, None]) & (padrow == 1)
        scores = jnp.where(valid[:, None, :], scores, -1e30)
        return lax.dynamic_update_slice_in_dim(buffer, scores, start, 2)

    empty_scores = jnp.full((rows, heads_here, ctx_slots), -1e30, jnp.float32)
    all_scores = lax.fori_loop(0, count, score_pass, empty_scores)
    top = jnp.maximum(jnp.max(all_scores, axis=-1), own)
    expo = jnp.where(all_scores > -1e29, jnp.exp(all_scores - top[..., None]), 0.0)
    own_exp = jnp.exp(own - top)
    total = jnp.sum(expo, axis=-1) + own_exp
    probs = (expo / total[..., None]).astype(jnp.bfloat16)
    own_prob = (own_exp / total).astype(jnp.bfloat16)

    def value_pass(step, acc):
        start = step * block
        pblock = lax.dynamic_slice_in_dim(probs, start, block, 2)
        vblock = lax.dynamic_slice_in_dim(v_cache, start, block, 2).reshape(
            rows, heads_here, HEAD_DIM, block
        )
        return acc + jnp.einsum("rhb,rhdb->rhd", pblock, vblock, preferred_element_type=jnp.float32)

    start_acc = own_prob.astype(jnp.float32)[..., None] * value_new.astype(jnp.float32)
    attn = (
        lax.fori_loop(0, count, value_pass, start_acc)
        .astype(jnp.bfloat16)
        .reshape(rows, local_width)
    )
    attn_terms = jnp.dot(attn, w_out, preferred_element_type=jnp.float32)
    resid = xvals + lax.psum(attn_terms, "tp")
    normed2 = rms_gain(resid, gain_mlp).astype(jnp.bfloat16)
    hidden = jax.nn.gelu(project_rows(normed2, w_up), approximate=True).astype(jnp.bfloat16)
    mlp_terms = jnp.dot(hidden, w_down, preferred_element_type=jnp.float32)
    state = (resid + lax.psum(mlp_terms, "tp")).astype(jnp.bfloat16)
    head = project_rows(state, w_head)
    pair_count = placement.shape[1]
    pairs_here = guide.shape[0]
    req_index = lax.axis_index("req")
    every_row = lax.all_gather(head, "req", axis=0, tiled=True)
    first = lax.dynamic_slice_in_dim(placement[0], req_index * pairs_here, pairs_here, 0)
    second = lax.dynamic_slice_in_dim(placement[1], req_index * pairs_here, pairs_here, 0)
    cond = jnp.take(every_row, first, axis=0)
    uncond = jnp.take(every_row, second + pair_count, axis=0)
    return uncond + guide[:, None] * (cond - uncond)


def solution(mesh):
    placed = (
        P("req", None),
        P(),
        P(None, "tp", None),
        P("req", "tp", None),
        P("req", "tp", None),
        P("req"),
        P("req", None),
        P("tp", None),
        P(),
        P("tp", None),
        P("tp", None),
        P("tp", None),
        P(),
        P("req"),
    )
    return jax.shard_map(
        on_device, mesh=mesh, in_specs=placed, out_specs=P("req", "tp"), check_vma=False
    )
```

profile of v0, /device:TPU:2, one launch (start us, length us, event | category | flops | bytes accessed | tf_op | source)
XLA Modules:
  0.0 116.9 jit_solution(2807817556014259598)
XLA Ops:
  0.0 0.9 fusion.17
  0.9 1.2 %convolution_convert_fusion.2 = bf16[4,160]{1,0:T(4,128)(2,1)S(1)} fusion(bf16[3,160,1280]{2,1,0:T(8,128)(2,1)} %param.22, bf16[4,1280]{1,0:T(4,128)(2,1)} %param.20, f32[1280]{0:T(1024)} %param.21, f32[4]{0:T(128)S(1)} %add_rsqrt_fusion.1), kind=kOutput, calls=%fused_computation.21 | convolution fusion | flops 1659520 | bytes 429328 | tf_op jit(solution)/shard_map/dot_general | solution.py:14
  2.1 0.1 reshape.85
  2.2 0.1 broadcast_in_dim.57
  2.3 8.8 %while.28 = (s32[]{:T(128)}, f32[4,2,2048]{2,1,0:T(2,128)S(1)}, s32[4]{0:T(128)}, s32[4,2048]{1,0:T(4,128)}, bf16[4,160,2048]{2,1,0:T(8,128)(2,1)}, /*index=5*/b...) while((s32[]{:T(128)}, f32[4,2,2048]{2,1,0:T(2,128)S(1)}, ...), condition=%wide.region_3.4_spmd.clone, body=%wide.region_2.3_spmd.clone.sunk | while | flops 670214 | bytes 2033075 | solution.py:68
  2.4 0.9 fusion.71
  3.2 1.1 constant_dynamic-slice_fusion.5
  4.4 0.2 fusion.70
  4.6 0.8 fusion.71
  5.4 1.1 constant_dynamic-slice_fusion.5
  6.5 0.2 fusion.70
  6.8 0.8 fusion.71
  7.6 1.1 constant_dynamic-slice_fusion.5
  8.7 0.2 fusion.70
  9.0 0.8 fusion.71
  9.8 1.1 constant_dynamic-slice_fusion.5
  10.9 0.2 fusion.70
  11.1 0.1 reduce_max.9
  11.2 0.2 fusion.10
  11.4 0.1 reshape.87
  11.5 0.2 multiply_reduce_fusion.1
  11.7 0.2 fusion.32
  11.9 0.1 divide_convert_fusion
  12.1 0.2 fusion.9
  12.3 0.1 reshape.88
  12.4 0.1 broadcast_multiply_fusion
  12.4 0.0 copy-start.1
  12.5 5.9 %while.27 = (s32[]{:T(128)}, f32[4,2,80]{2,1,0:T(2,128)S(1)}, bf16[4,2,2048]{2,1,0:T(2,128)(2,1)S(1)}, bf16[4,160,2048]{2,1,0:T(8,128)(2,1)}, s32[]{:T(128)}, /*index=5*/s32[]{:T(128)}, s32[]{:T(128)}, s32[]{:T(128)}) while((s32[]{:T(128)}, f32[4,2,80]{2,1,0:T(2,128)S(1)}, bf16[4,2,2048]{2,1,0:T(2,128)(2,1)S(1)}, ...), condition=%wide.region_7.8_spmd, body=%wide.region_6.7_spmd.sunk | while | flops 656006 | bytes 2001035 | solution.py:86
  12.5 1.2 %constant_dynamic-slice_fusion.4 = bf16[4,160,512]{2,1,0:T(8,128)(2,1)S(1)} fusion(bf16[4,160,2048]{2,1,0:T(8,128)(2,1)} %get-tuple-element.366, s32[]{:T(128)S(6)} %select_n.71), kind=kLoop, calls=%fused_computation.6.clone.1 | loop fusion | bytes 1310724 | tf_op jit(solution)/shard_map/while/body/eval_jaxpr/dynamic_slice | solution.py:79
  13.8 0.3 fusion.67
  14.1 1.1 constant_dynamic-slice_fusion.4
  15.2 0.3 fusion.67
  15.5 1.1 constant_dynamic-slice_fusion.4
  16.7 0.3 fusion.67
  17.0 1.1 constant_dynamic-slice_fusion.4
  18.1 0.3 fusion.67
  18.5 0.1 reshape.86
  18.6 0.2 fusion.49
  18.7 25.9 %psum.14 = f32[4,1280]{1,0:T(4,128)S(1)} all-reduce(f32[4,1280]{1,0:T(4,128)S(1)} %fusion.49), channel_id=1, replica_groups=mesh['req'=32,'tp'=8] {'tp'}, use_global_device_ids=true, to_apply=%region_8.9 | all-reduce | flops 5120 | bytes 40960 | tf_op jit(solution)/shard_map/psum | solution.py:91
  44.6 0.1 multiply_reduce_fusion
  44.8 0.5 fusion.31
  45.3 23.6 %psum.15 = f32[4,1280]{1,0:T(4,128)S(1)} all-reduce(f32[4,1280]{1,0:T(4,128)S(1)} %fusion.31), channel_id=1, replica_groups=mesh['req'=32,'tp'=8] {'tp'}, use_global_device_ids=true, to_apply=%region_10.11 | all-reduce | flops 5120 | bytes 40960 | tf_op jit(solution)/shard_map/psum | solution.py:95
  68.9 0.2 convolution_bitcast_fusion
  69.0 45.9 %all-gather = f32[32,4,160]{2,1,0:T(4,128)S(1)} all-gather(f32[1,4,160]{2,1,0:T(4,128)S(1)} %convolution_bitcast_fusion), channel_id=1, replica_groups=mesh['req'=32,'tp'=8] {'req'}, dimensions={0}, use_global_device_ids=true | all-gather | bytes 84480 | tf_op jit(solution)/shard_map/all_gather | solution.py:100
  115.0 0.1 compare_and_fusion
  115.1 0.6 gather_fusion
  115.7 0.6 gather_fusion.1
  116.3 0.7 fusion.34
  (44 shorter events, 0.4 us)
Async XLA Ops:
  0.0 18.6 %copy-start = (bf16[160,1280]{1,0:T(8,128)(2,1)S(1)}, bf16[160,1280]{1,0:T(8,128)(2,1)}, u32[]{:S(2)}) copy-start(bf16[160,1280]{1,0:T(8,128)(2,1)} %param.27) | copy-start | bytes 1228804
  2.3 8.9 %copy-start.4 = (bf16[4,1280]{1,0:T(4,128)(2,1)S(1)}, bf16[4,1280]{1,0:T(4,128)(2,1)}, u32[]{:S(2)}) copy-start(bf16[4,1280]{1,0:T(4,128)(2,1)} %param.20) | copy-start | bytes 30724
  2.3 8.9 %copy-start.8 = (bf16[3,160,1280]{2,1,0:T(8,128)(2,1)S(1)}, bf16[3,160,1280]{2,1,0:T(8,128)(2,1)}, u32[]{:S(2)}) copy-start(bf16[3,160,1280]{2,1,0:T(8,128)(2,1)} %param.22) | copy-start | bytes 3686404
  2.3 8.9 %copy-start.9 = (f32[1280]{0:T(1024)S(1)}, f32[1280]{0:T(1024)}, u32[]{:S(2)}) copy-start(f32[1280]{0:T(1024)} %param.21) | copy-start | bytes 15364
  12.4 32.3 %copy-start.1 = (bf16[160,1280]{1,0:T(8,128)(2,1)S(1)}, bf16[160,1280]{1,0:T(8,128)(2,1)}, u32[]{:S(2)}) copy-start(bf16[160,1280]{1,0:T(8,128)(2,1)} %param.30) | copy-start | bytes 1228804
  12.5 32.3 %copy-start.2 = (bf16[160,1280]{1,0:T(8,128)(2,1)S(1)}, bf16[160,1280]{1,0:T(8,128)(2,1)}, u32[]{:S(2)}) copy-start(bf16[160,1280]{1,0:T(8,128)(2,1)} %param.29) | copy-start | bytes 1228804
  12.5 32.3 %copy-start.5 = (f32[1280]{0:T(1024)S(1)}, f32[1280]{0:T(1024)}, u32[]{:S(2)}) copy-start(f32[1280]{0:T(1024)} %param.28) | copy-start | bytes 15364
  18.4 50.5 %copy-start.3 = (bf16[160,1280]{1,0:T(8,128)(2,1)S(1)}, bf16[160,1280]{1,0:T(8,128)(2,1)}, u32[]{:S(2)}) copy-start(bf16[160,1280]{1,0:T(8,128)(2,1)} %param.31) | copy-start | bytes 1228804
  18.4 96.6 %copy-start.6 = (s32[2,64]{1,0:T(2,128)S(1)}, s32[2,64]{1,0:T(2,128)}, u32[]{:S(2)}) copy-start(s32[2,64]{1,0:T(2,128)} %param.32) | copy-start | bytes 1540
  18.4 97.8 %copy-start.7 = (f32[2]{0:T(128)S(1)}, f32[2]{0:T(128)}, u32[]{:S(2)}) copy-start(f32[2]{0:T(128)} %param.33) | copy-start | bytes 28
where the time goes:
time: 118 us; the launch traced here: 117 us
  blocking collectives  95.4 us (81%)
  local copies, waits for them, and re-layouts  10.9 us (9%)
  other arithmetic  5.9 us (5%)
  matrix products  4.29 us (4%)
    all_gather x1, blocking collectives, on_device(): every_row = lax.all_gather(head, 'req', axis=0, tiled=True)  45.9 us
    psum x1, blocking collectives, on_device(): resid = xvals + lax.psum(attn_terms, 'tp')  25.9 us
    psum x1, blocking collectives, on_device(): state = (resid + lax.psum(mlp_terms, 'tp')).astype(jnp.bfloat16)  23.6 us
    dynamic_slice x4, local copies, waits for them, and re-layouts, value_pass(): lax.dynamic_slice_in_dim(v_cache, start, block, 2)  4.64 us
    dynamic_slice x4, local copies, waits for them, and re-layouts, score_pass(): lax.dynamic_slice_in_dim(k_cache, start, block, 2)  4.52 us
    and x4, other arithmetic, score_pass(): valid = ((start + offsets)[None, :] < lengths[:, None]) & (padrow == 1)  3.2 us

commit v1 on v0

--- a/solution.py
+++ b/solution.py
@@ -14,6 +14,11 @@
     return lax.dot_general(
         left, weight, (((1,), (1,)), ((), ())), preferred_element_type=jnp.float32
     )
+
+
+def tp_sum(part):
+    copies = jnp.broadcast_to(part.astype(jnp.bfloat16)[None], (lax.axis_size("tp"),) + part.shape)
+    return jnp.sum(lax.all_to_all(copies, "tp", 0, 0).astype(jnp.float32), axis=0)
 
 
 def on_device(
@@ -88,20 +93,23 @@
         .reshape(rows, local_width)
     )
     attn_terms = jnp.dot(attn, w_out, preferred_element_type=jnp.float32)
-    resid = xvals + lax.psum(attn_terms, "tp")
+    resid = xvals + tp_sum(attn_terms)
     normed2 = rms_gain(resid, gain_mlp).astype(jnp.bfloat16)
     hidden = jax.nn.gelu(project_rows(normed2, w_up), approximate=True).astype(jnp.bfloat16)
     mlp_terms = jnp.dot(hidden, w_down, preferred_element_type=jnp.float32)
-    state = (resid + lax.psum(mlp_terms, "tp")).astype(jnp.bfloat16)
+    state = (resid + tp_sum(mlp_terms)).astype(jnp.bfloat16)
     head = project_rows(state, w_head)
-    pair_count = placement.shape[1]
     pairs_here = guide.shape[0]
+    req_count = lax.axis_size("req")
+    half = req_count // 2
     req_index = lax.axis_index("req")
-    every_row = lax.all_gather(head, "req", axis=0, tiled=True)
-    first = lax.dynamic_slice_in_dim(placement[0], req_index * pairs_here, pairs_here, 0)
-    second = lax.dynamic_slice_in_dim(placement[1], req_index * pairs_here, pairs_here, 0)
-    cond = jnp.take(every_row, first, axis=0)
-    uncond = jnp.take(every_row, second + pair_count, axis=0)
+    wanted = jnp.where(req_index < half, placement[0], placement[1])
+    mine = (req_index % half) * rows + jnp.arange(rows, dtype=jnp.int32)
+    picked = jnp.sum(jnp.where((wanted[:, None] == mine[None, :])[:, :, None], head[None], 0.0), axis=1)
+    slots = picked.reshape(req_count, pairs_here, head.shape[1])
+    arrived = lax.all_to_all(slots, "req", 0, 0)
+    cond = jnp.sum(arrived[:half], axis=0)
+    uncond = jnp.sum(arrived[half:], axis=0)
     return uncond + guide[:, None] * (cond - uncond)
 
 

time: 118 us -> 64.4 us (0.55)
  blocking collectives: 95.4 us -> 20.3 us
  waiting for transfers between devices: 0 us -> 11.2 us
  starting transfers between devices: 0 us -> 7.96 us
  matrix products: 4.29 us -> 6.51 us
    psum x2 -> x0, blocking collectives: 49.5 us -> none  [the longest x1 25.9 us: on_device(): resid = xvals + lax.psum(attn_terms, 'tp')]
    all_gather x1 -> x0, blocking collectives: 45.9 us -> none  [on_device(): every_row = lax.all_gather(head, 'req', axis=0, tiled=True)]
    all_to_all x0 -> x1, blocking collectives: none -> 20.3 us  [on_device(): arrived = lax.all_to_all(slots, 'req', 0, 0)]
    all_to_all x0 -> x2, waiting for transfers between devices: none -> 11.2 us  [tp_sum(): lax.all_to_all(copies, 'tp', 0, 0).astype(jnp.float32)]
    all_to_all x0 -> x2, starting transfers between devices: none -> 7.96 us  [tp_sum(): lax.all_to_all(copies, 'tp', 0, 0).astype(jnp.float32)]
    dot_general x4, matrix products: 1.79 us -> 4.01 us  [project_rows(): lax.dot_general(left, weight, (((1,), (1,)), ((), ())), preferred_element...]
    broadcast_in_dim x0 -> x2, local copies, waits for them, and re-layouts: none -> 1.32 us  [tp_sum(): jnp.broadcast_to(part.astype(jnp.bfloat16)[None], (lax.axis_size('tp'),)...]
  transfers between devices with their start and end apart: 0 -> 2, of which waited for: 0 -> 2; matrix products, arithmetic and copies ran while one was open for 0% -> 0% of each run, Pallas kernels for 0% -> 0%
where the time goes in v1:
time: 64.4 us; the launch traced here: 63.4 us
  blocking collectives  20.3 us (32%)
  waiting for transfers between devices  11.2 us (17%)
  local copies, waits for them, and re-layouts  11.1 us (17%)
  starting transfers between devices  7.96 us (12%)
  matrix products  6.51 us (10%)
  other arithmetic  6.05 us (9%)
    all_to_all x1, blocking collectives, on_device(): arrived = lax.all_to_all(slots, 'req', 0, 0)  20.3 us
    all_to_all x2, waiting for transfers between devices, tp_sum(): lax.all_to_all(copies, 'tp', 0, 0).astype(jnp.float32)  11.2 us
    all_to_all x2, starting transfers between devices, tp_sum(): lax.all_to_all(copies, 'tp', 0, 0).astype(jnp.float32)  7.96 us
    dynamic_slice x4, local copies, waits for them, and re-layouts, value_pass(): lax.dynamic_slice_in_dim(v_cache, start, block, 2)  4.65 us
    dynamic_slice x4, local copies, waits for them, and re-layouts, score_pass(): lax.dynamic_slice_in_dim(k_cache, start, block, 2)  4.52 us
    dot_general x4, matrix products, project_rows(): lax.dot_general(left, weight, (((1,), (1,)), ((), ())), preferred_element...  4.01 us
    and x4, other arithmetic, score_pass(): valid = ((start + offsets)[None, :] < lengths[:, None]) & (padrow == 1)  3.1 us
    broadcast_in_dim x2, local copies, waits for them, and re-layouts, tp_sum(): jnp.broadcast_to(part.astype(jnp.bfloat16)[None], (lax.axis_size('tp'),)...  1.32 us
  transfers between devices with their start and end apart: 2, of which 2 were waited for; matrix products, arithmetic and copies ran while one was open for 0% of the time, Pallas kernels for 0%

profile of v1, /device:TPU:2, one launch (start us, length us, event | category | flops | bytes accessed | tf_op | source)
XLA Modules:
  0.0 63.4 jit_solution(11847502493536010019)
XLA Ops:
  0.0 0.9 %fusion.17 = f32[4]{0:T(128)S(1)} fusion(bf16[4,1280]{1,0:T(4,128)(2,1)} %param.18), kind=kLoop, calls=%fused_computation.37 | loop fusion | flops 15356 | bytes 10256 | tf_op jit(solution)/shard_map/reduce_sum | solution.py:10
  0.9 1.2 %convolution_convert_fusion.4 = bf16[4,160]{1,0:T(4,128)(2,1)S(1)} fusion(bf16[3,160,1280]{2,1,0:T(8,128)(2,1)} %param.20, bf16[4,1280]{1,0:T(4,128)(2,1)} %param.18, f32[1280]{0:T(1024)} %param.19, f32[4]{0:T(128)S(1)} %add_rsqrt_fusion.1), kind=kOutput, calls=%fused_computation.20 | convolution fusion | flops 1659520 | bytes 429328 | tf_op jit(solution)/shard_map/dot_general | solution.py:14
  2.1 1.3 %fusion.10 = f32[4,160]{1,0:T(4,128)S(1)} fusion(bf16[3,160,1280]{2,1,0:T(8,128)(2,1)} %param.20, bf16[4,1280]{1,0:T(4,128)(2,1)} %param.18, f32[1280]{0:T(1024)} %param.19, f32[4]{0:T(128)S(1)} %add_rsqrt_fusion.1), kind=kOutput, calls=%fused_computation.19 | convolution fusion | flops 1660160 | bytes 430608 | tf_op jit(solution)/shard_map/dot_general | solution.py:14
  3.4 1.3 %fusion.9 = f32[4,160]{1,0:T(4,128)S(1)} fusion(bf16[3,160,1280]{2,1,0:T(8,128)(2,1)} %param.20, bf16[4,1280]{1,0:T(4,128)(2,1)} %param.18, f32[1280]{0:T(1024)} %param.19, f32[4]{0:T(128)S(1)} %add_rsqrt_fusion.1), kind=kOutput, calls=%fused_computation.17 | convolution fusion | flops 1660160 | bytes 430608 | tf_op jit(solution)/shard_map/dot_general | solution.py:14
  4.7 0.1 reshape.124
  4.8 0.1 broadcast_in_dim.85
  4.9 8.7 %while.28 = (s32[]{:T(128)}, f32[4,2,2048]{2,1,0:T(2,128)S(1)}, s32[4]{0:T(128)S(1)}, s32[4,2048]{1,0:T(4,128)}, bf16[4,160,2048]{2,1,0:T(8,128)(2,1)}, /*index=...) while((s32[]{:T(128)}, f32[4,2,2048]{2,1,0:T(2,128)S(1)}, ...), condition=%wide.region_3.4_spmd.clone, body=%wide.region_2.3_spmd.clone.sunk | while | flops 670214 | bytes 2033075 | solution.py:73
  5.0 0.8 %fusion.68 = pred[4,512]{1,0:T(4,128)(4,1)S(1)} fusion(s32[4,2048]{1,0:T(4,128)} %get-tuple-element.333, s32[]{:T(128)S(6)} %select_n.83, s32[512]{0:T(512)S(1)} %iota_add_fusion.3, s32[4]{0:T(128)S(1)} %get-tuple-element.332), kind=kLoop, calls=%fused_computation.9.clone.1 | loop fusion | flops 6144 | bytes 12308 | tf_op jit(solution)/shard_map/while/body/eval_jaxpr/and | solution.py:68
  5.7 1.1 %constant_dynamic-slice_fusion.5 = bf16[4,160,512]{2,1,0:T(8,128)(2,1)S(1)} fusion(bf16[4,160,2048]{2,1,0:T(8,128)(2,1)} %get-tuple-element.334, s32[]{:T(128)S(6)} %select_n.83), kind=kLoop, calls=%fused_computation.13.clone.1 | loop fusion | bytes 1310724 | tf_op jit(solution)/shard_map/while/body/eval_jaxpr/dynamic_slice | solution.py:61
  6.9 0.2 fusion.67
  7.1 0.8 %fusion.68 = pred[4,512]{1,0:T(4,128)(4,1)S(1)} fusion(s32[4,2048]{1,0:T(4,128)} %get-tuple-element.333, s32[]{:T(128)S(6)} %select_n.83, s32[512]{0:T(512)S(1)} %iota_add_fusion.3, s32[4]{0:T(128)S(1)} %get-tuple-element.332), kind=kLoop, calls=%fused_computation.9.clone.1 | loop fusion | flops 6144 | bytes 12308 | tf_op jit(solution)/shard_map/while/body/eval_jaxpr/and | solution.py:68
  7.9 1.1 %constant_dynamic-slice_fusion.5 = bf16[4,160,512]{2,1,0:T(8,128)(2,1)S(1)} fusion(bf16[4,160,2048]{2,1,0:T(8,128)(2,1)} %get-tuple-element.334, s32[]{:T(128)S(6)} %select_n.83), kind=kLoop, calls=%fused_computation.13.clone.1 | loop fusion | bytes 1310724 | tf_op jit(solution)/shard_map/while/body/eval_jaxpr/dynamic_slice | solution.py:61
  9.0 0.2 fusion.67
  9.3 0.8 %fusion.68 = pred[4,512]{1,0:T(4,128)(4,1)S(1)} fusion(s32[4,2048]{1,0:T(4,128)} %get-tuple-element.333, s32[]{:T(128)S(6)} %select_n.83, s32[512]{0:T(512)S(1)} %iota_add_fusion.3, s32[4]{0:T(128)S(1)} %get-tuple-element.332), kind=kLoop, calls=%fused_computation.9.clone.1 | loop fusion | flops 6144 | bytes 12308 | tf_op jit(solution)/shard_map/while/body/eval_jaxpr/and | solution.py:68
  10.1 1.1 %constant_dynamic-slice_fusion.5 = bf16[4,160,512]{2,1,0:T(8,128)(2,1)S(1)} fusion(bf16[4,160,2048]{2,1,0:T(8,128)(2,1)} %get-tuple-element.334, s32[]{:T(128)S(6)} %select_n.83), kind=kLoop, calls=%fused_computation.13.clone.1 | loop fusion | bytes 1310724 | tf_op jit(solution)/shard_map/while/body/eval_jaxpr/dynamic_slice | solution.py:61
  11.2 0.2 fusion.67
  11.5 0.8 %fusion.68 = pred[4,512]{1,0:T(4,128)(4,1)S(1)} fusion(s32[4,2048]{1,0:T(4,128)} %get-tuple-element.333, s32[]{:T(128)S(6)} %select_n.83, s32[512]{0:T(512)S(1)} %iota_add_fusion.3, s32[4]{0:T(128)S(1)} %get-tuple-element.332), kind=kLoop, calls=%fused_computation.9.clone.1 | loop fusion | flops 6144 | bytes 12308 | tf_op jit(solution)/shard_map/while/body/eval_jaxpr/and | solution.py:68
  12.2 1.1 %constant_dynamic-slice_fusion.5 = bf16[4,160,512]{2,1,0:T(8,128)(2,1)S(1)} fusion(bf16[4,160,2048]{2,1,0:T(8,128)(2,1)} %get-tuple-element.334, s32[]{:T(128)S(6)} %select_n.83), kind=kLoop, calls=%fused_computation.13.clone.1 | loop fusion | bytes 1310724 | tf_op jit(solution)/shard_map/while/body/eval_jaxpr/dynamic_slice | solution.py:61
  13.4 0.2 fusion.67
  13.6 0.1 reshape.127
  13.7 0.1 multiply_reduce_fusion.1
  13.8 0.1 reduce_max.9
  13.9 0.2 fusion.32
  14.1 0.1 divide_convert_fusion
  14.3 0.1 reshape.128
  14.5 5.9 %while.27 = (s32[]{:T(128)}, f32[4,2,80]{2,1,0:T(2,128)S(1)}, bf16[4,2,2048]{2,1,0:T(2,128)(2,1)S(1)}, bf16[4,160,2048]{2,1,0:T(8,128)(2,1)}, s32[]{:T(128)}, /*index=5*/s32[]{:T(128)}, s32[]{:T(128)}, s32[]{:T(128)}) while((s32[]{:T(128)}, f32[4,2,80]{2,1,0:T(2,128)S(1)}, bf16[4,2,2048]{2,1,0:T(2,128)(2,1)S(1)}, ...), condition=%wide.region_7.8_spmd, body=%wide.region_6.7_spmd.sunk | while | flops 656006 | bytes 2001035 | solution.py:91
  14.5 1.2 %constant_dynamic-slice_fusion.4 = bf16[4,160,512]{2,1,0:T(8,128)(2,1)S(1)} fusion(bf16[4,160,2048]{2,1,0:T(8,128)(2,1)} %get-tuple-element.359, s32[]{:T(128)S(6)} %select_n.81), kind=kLoop, calls=%fused_computation.4.clone.1 | loop fusion | bytes 1310724 | tf_op jit(solution)/shard_map/while/body/eval_jaxpr/dynamic_slice | solution.py:84
  15.7 0.3 fusion.64
  16.0 1.1 %constant_dynamic-slice_fusion.4 = bf16[4,160,512]{2,1,0:T(8,128)(2,1)S(1)} fusion(bf16[4,160,2048]{2,1,0:T(8,128)(2,1)} %get-tuple-element.359, s32[]{:T(128)S(6)} %select_n.81), kind=kLoop, calls=%fused_computation.4.clone.1 | loop fusion | bytes 1310724 | tf_op jit(solution)/shard_map/while/body/eval_jaxpr/dynamic_slice | solution.py:84
  17.2 0.3 fusion.64
  17.5 1.1 %constant_dynamic-slice_fusion.4 = bf16[4,160,512]{2,1,0:T(8,128)(2,1)S(1)} fusion(bf16[4,160,2048]{2,1,0:T(8,128)(2,1)} %get-tuple-element.359, s32[]{:T(128)S(6)} %select_n.81), kind=kLoop, calls=%fused_computation.4.clone.1 | loop fusion | bytes 1310724 | tf_op jit(solution)/shard_map/while/body/eval_jaxpr/dynamic_slice | solution.py:84
  18.6 0.3 fusion.64
  18.9 1.1 %constant_dynamic-slice_fusion.4 = bf16[4,160,512]{2,1,0:T(8,128)(2,1)S(1)} fusion(bf16[4,160,2048]{2,1,0:T(8,128)(2,1)} %get-tuple-element.359, s32[]{:T(128)S(6)} %select_n.81), kind=kLoop, calls=%fused_computation.4.clone.1 | loop fusion | bytes 1310724 | tf_op jit(solution)/shard_map/while/body/eval_jaxpr/dynamic_slice | solution.py:84
  20.1 0.3 fusion.64
  20.4 0.1 reshape.125
  20.5 0.2 convolution_convert_fusion.1
  20.7 0.7 %broadcast_in_dim.87 = bf16[8,4,1280]{2,1,0:T(4,128)(2,1)} broadcast(bf16[4,1280]{1,0:T(4,128)(2,1)S(1)} %convolution_convert_fusion.1), dimensions={1,2} | broadcast | bytes 92160 | tf_op jit(solution)/shard_map/broadcast_in_dim | solution.py:20
  21.3 4.6 %all-to-all-start = ((bf16[8,4,1280]{2,1,0:T(4,128)(2,1)}), bf16[8,4,1280]{2,1,0:T(4,128)(2,1)S(1)}, u32[]{:S(2)}, u32[]{:S(2)}) async-start(bf16[8,4,1280]{2,1,0:T(4,128)(2,1)} %broadcast_in_dim.87), calls=%async_computation | async-start | bytes 163840 | tf_op jit(solution)/shard_map/all_to_all | solution.py:21
  26.0 5.7 %all-to-all-done = bf16[8,4,1280]{2,1,0:T(4,128)(2,1)S(1)} async-done(((bf16[8,4,1280]{2,1,0:T(4,128)(2,1)}), bf16[8,4,1280]{2,1,0:T(4,128)(2,1)S(1)}, u32[]{:S(2)}, u32[]{:S(2)}) %all-to-all-start) | async-done | bytes 81952 | tf_op jit(solution)/shard_map/all_to_all | solution.py:21
  31.7 0.1 multiply_reduce_fusion
  31.9 0.5 convolution_convert_fusion
  32.4 0.7 %broadcast_in_dim.88 = bf16[8,4,1280]{2,1,0:T(4,128)(2,1)} broadcast(bf16[4,1280]{1,0:T(4,128)(2,1)S(1)} %convolution_convert_fusion), dimensions={1,2} | broadcast | bytes 92160 | tf_op jit(solution)/shard_map/broadcast_in_dim | solution.py:20
  33.0 3.4 %all-to-all-start.1 = ((bf16[8,4,1280]{2,1,0:T(4,128)(2,1)}), bf16[8,4,1280]{2,1,0:T(4,128)(2,1)S(1)}, u32[]{:S(2)}, u32[]{:S(2)}) async-start(bf16[8,4,1280]{2,1,0:T(4,128)(2,1)} %broadcast_in_dim.88), calls=%async_computation.1 | async-start | bytes 163840 | tf_op jit(solution)/shard_map/all_to_all | solution.py:21
  36.5 5.6 %all-to-all-done.1 = bf16[8,4,1280]{2,1,0:T(4,128)(2,1)S(1)} async-done(((bf16[8,4,1280]{2,1,0:T(4,128)(2,1)}), bf16[8,4,1280]{2,1,0:T(4,128)(2,1)S(1)}, u32[]{:S(2)}, u32[]{:S(2)}) %all-to-all-start.1) | async-done | bytes 81952 | tf_op jit(solution)/shard_map/all_to_all | solution.py:21
  42.1 0.2 fusion.21
  42.3 0.2 select_reduce_fusion
  42.5 20.3 %all_to_all.15 = f32[32,2,160]{2,1,0:T(2,128)S(1)} all-to-all(f32[32,2,160]{2,1,0:T(2,128)S(1)} %reshape.126), channel_id=1, replica_groups=mesh['req'=32,'tp'=8] {'req'}, dimensions={0} | all-to-all | bytes 81920 | tf_op jit(solution)/shard_map/all_to_all | solution.py:110
  62.8 0.6 %multiply_add_fusion = f32[2,160]{1,0:T(2,128)} fusion(f32[2,160]{1,0:T(2,128)S(1)} %get-tuple-element.225, f32[2,160]{1,0:T(2,128)S(1)} %get-tuple-element.224, f32[2]{0:T(128)S(1)} %copy-done.8), kind=kLoop, calls=%fused_computation.58 | loop fusion | flops 960 | bytes 3848 | tf_op jit(solution)/shard_map/add | solution.py:113
  (47 shorter events, 0.7 us)
Async XLA Ops:
  0.0 20.5 %copy-start = (bf16[160,1280]{1,0:T(8,128)(2,1)S(1)}, bf16[160,1280]{1,0:T(8,128)(2,1)}, u32[]{:S(2)}) copy-start(bf16[160,1280]{1,0:T(8,128)(2,1)} %param.25) | copy-start | bytes 1228804
  0.0 4.9 %copy-start.5 = (s32[4]{0:T(128)S(1)}, s32[4]{0:T(128)}, u32[]{:S(2)}) copy-start(s32[4]{0:T(128)} %param.23) | copy-start | bytes 52
  14.4 11.5 %copy-start.7 = (s32[2,64]{1,0:T(2,128)S(1)}, s32[2,64]{1,0:T(2,128)}, u32[]{:S(2)}) copy-start(s32[2,64]{1,0:T(2,128)} %param.30) | copy-start | bytes 1540
  14.5 17.2 %copy-start.4 = (bf16[4,1280]{1,0:T(4,128)(2,1)S(1)}, bf16[4,1280]{1,0:T(4,128)(2,1)}, u32[]{:S(2)}) copy-start(bf16[4,1280]{1,0:T(4,128)(2,1)} %param.18) | copy-start | bytes 30724
  14.5 17.4 %copy-start.1 = (bf16[160,1280]{1,0:T(8,128)(2,1)S(1)}, bf16[160,1280]{1,0:T(8,128)(2,1)}, u32[]{:S(2)}) copy-start(bf16[160,1280]{1,0:T(8,128)(2,1)} %param.28) | copy-start | bytes 1228804
  14.5 17.4 %copy-start.2 = (bf16[160,1280]{1,0:T(8,128)(2,1)S(1)}, bf16[160,1280]{1,0:T(8,128)(2,1)}, u32[]{:S(2)}) copy-start(bf16[160,1280]{1,0:T(8,128)(2,1)} %param.27) | copy-start | bytes 1228804
  14.5 17.4 %copy-start.6 = (f32[1280]{0:T(1024)S(1)}, f32[1280]{0:T(1024)}, u32[]{:S(2)}) copy-start(f32[1280]{0:T(1024)} %param.26) | copy-start | bytes 15364
  20.4 21.7 %copy-start.3 = (bf16[160,1280]{1,0:T(8,128)(2,1)S(1)}, bf16[160,1280]{1,0:T(8,128)(2,1)}, u32[]{:S(2)}) copy-start(bf16[160,1280]{1,0:T(8,128)(2,1)} %param.29) | copy-start | bytes 1228804
  21.3 41.5 %copy-start.8 = (f32[2]{0:T(128)S(1)}, f32[2]{0:T(128)}, u32[]{:S(2)}) copy-start(f32[2]{0:T(128)} %param.31) | copy-start | bytes 28
  21.3 10.3 %all-to-all-start = ((bf16[8,4,1280]{2,1,0:T(4,128)(2,1)}), bf16[8,4,1280]{2,1,0:T(4,128)(2,1)S(1)}, u32[]{:S(2)}, u32[]{:S(2)}) async-start(bf16[8,4,1280]{2,1,0:T(4,128)(2,1)} %broadcast_in_dim.87), calls=%async_computation | async-start | bytes 163840 | tf_op jit(solution)/shard_map/all_to_all | solution.py:21
  33.0 9.0 %all-to-all-start.1 = ((bf16[8,4,1280]{2,1,0:T(4,128)(2,1)}), bf16[8,4,1280]{2,1,0:T(4,128)(2,1)S(1)}, u32[]{:S(2)}, u32[]{:S(2)}) async-start(bf16[8,4,1280]{2,1,0:T(4,128)(2,1)} %broadcast_in_dim.88), calls=%async_computation.1 | async-start | bytes 163840 | tf_op jit(solution)/shard_map/all_to_all | solution.py:21

commit v2 on v0

v2 whole, which is shorter than its diff:
```python
import functools

import jax
import jax.numpy as jnp
from jax import lax
from jax.experimental import pallas as pl
from jax.experimental.pallas import tpu as pltpu
from jax.sharding import PartitionSpec as P

HEAD_DIM = 80
NEG = -1e30
VMEM_BYTES = 40 << 20


def rms_gain(values, gain):
    return values * lax.rsqrt(jnp.mean(values * values, axis=-1, keepdims=True) + 1e-06) * gain


def rows_by_weight(left, weight):
    return lax.dot_general(
        left, weight, (((1,), (1,)), ((), ())), preferred_element_type=jnp.float32
    )


def spread(values, owner, count):
    out = jnp.broadcast_to(values[0:1], owner.shape)
    for r in range(1, count):
        out = jnp.where(owner == r, jnp.broadcast_to(values[r : r + 1], owner.shape), out)
    return out


def attend_kernel(
    x_hbm,
    gain_hbm,
    w_hbm,
    k_hbm,
    v_hbm,
    len_hbm,
    pad_hbm,
    wo_hbm,
    out_ref,
    x_v,
    gain_v,
    w_v,
    k_v,
    v_v,
    len_s,
    pad_v,
    wo_v,
    sems,
):
    rows, width, slots = k_v.shape
    heads = width // HEAD_DIM
    many = rows * heads
    copies = [
        (x_hbm, x_v),
        (gain_hbm, gain_v),
        (w_hbm.at[0], w_v.at[0]),
        (len_hbm, len_s),
        (pad_hbm, pad_v),
    ]
    copies += [(k_hbm.at[r], k_v.at[r]) for r in range(rows)]
    copies += [(w_hbm.at[1], w_v.at[1]), (w_hbm.at[2], w_v.at[2])]
    copies += [(v_hbm.at[r], v_v.at[r]) for r in range(rows)]
    copies += [(wo_hbm, wo_v)]
    flights = [pltpu.make_async_copy(a, b, sems.at[i]) for i, (a, b) in enumerate(copies)]
    for flight in flights:
        flight.start()
    x_in, gain_in, wq_in, len_in, pad_in = flights[:5]
    k_in = flights[5 : 5 + rows]
    wk_in, wv_in = flights[5 + rows : 7 + rows]
    v_in = flights[7 + rows : 7 + 2 * rows]
    wo_in = flights[7 + 2 * rows]
    scale = HEAD_DIM ** (-0.5)

    row_n = lax.broadcasted_iota(jnp.int32, (many, width), 0)
    col_n = lax.broadcasted_iota(jnp.int32, (many, width), 1)
    owner_n = row_n // heads
    own_head = col_n // HEAD_DIM == row_n % heads
    x_in.wait()
    gain_in.wait()
    normed = rms_gain(x_v[...].astype(jnp.float32), gain_v[...]).astype(jnp.bfloat16)

    len_in.wait()
    pad_in.wait()
    row_w = lax.broadcasted_iota(jnp.int32, (many, slots), 0) // heads
    col_w = lax.broadcasted_iota(jnp.int32, (many, slots), 1)
    filled = jnp.full((many, slots), len_s[0], jnp.int32)
    for r in range(1, rows):
        filled = jnp.where(row_w == r, len_s[r], filled)
    valid = (col_w < filled) & (spread(pad_v[...], row_w, rows) == 1)

    def project(which):
        flat = rows_by_weight(normed, w_v[which])
        return spread(flat.astype(jnp.bfloat16).astype(jnp.float32), owner_n, rows)

    wq_in.wait()
    query = jnp.where(own_head, project(0), 0.0)
    scores = None
    for r in range(rows):
        picked = jnp.where(owner_n == r, query, 0.0).astype(jnp.bfloat16)
        k_in[r].wait()
        part = jnp.dot(picked, k_v[r], preferred_element_type=jnp.float32)
        scores = part if scores is None else scores + part
    scores = jnp.where(valid, scores * scale, NEG)
    wk_in.wait()
    own = jnp.sum(query * project(1), axis=1, keepdims=True) * scale
    wv_in.wait()
    value_new = project(2)
    top = jnp.maximum(jnp.max(scores, axis=1, keepdims=True), own)
    expo = jnp.where(valid, jnp.exp(scores - top), 0.0)
    own_exp = jnp.exp(own - top)
    total = jnp.sum(expo, axis=1, keepdims=True) + own_exp
    probs = (expo / total).astype(jnp.bfloat16)
    own_prob = (own_exp / total).astype(jnp.bfloat16).astype(jnp.float32)
    mixed = own_prob * value_new
    for r in range(rows):
        v_in[r].wait()
        mixed = mixed + jnp.where(owner_n == r, rows_by_weight(probs, v_v[r]), 0.0)
    mixed = jnp.where(own_head, mixed, 0.0).astype(jnp.bfloat16).astype(jnp.float32)
    attn = mixed
    for h in range(1, heads):
        attn = attn + pltpu.roll(mixed, many - h, 0)
    wo_in.wait()
    terms = jnp.dot(attn.astype(jnp.bfloat16), wo_v[...], preferred_element_type=jnp.float32)
    terms = jnp.concatenate([terms[r * heads : r * heads + 1] for r in range(rows)], axis=0)
    terms = terms.astype(out_ref.dtype)
    for t in range(out_ref.shape[0]):
        out_ref[t] = terms


def mlp_kernel(parts_ref, x_ref, gain_ref, up_ref, down_ref, out_ref, resid_ref):
    resid = x_ref[...].astype(jnp.float32) + jnp.sum(parts_ref[...].astype(jnp.float32), axis=0)
    resid_ref[...] = resid
    normed = rms_gain(resid, gain_ref[...]).astype(jnp.bfloat16)
    hidden = jax.nn.gelu(rows_by_weight(normed, up_ref[...]), approximate=True)
    terms = jnp.dot(hidden.astype(jnp.bfloat16), down_ref[...], preferred_element_type=jnp.float32)
    terms = terms.astype(out_ref.dtype)
    for t in range(out_ref.shape[0]):
        out_ref[t] = terms


def head_kernel(parts_ref, resid_ref, head_ref, place_ref, out_ref, *, half):
    rows = resid_ref.shape[0]
    pairs = place_ref.shape[1]
    total = jnp.sum(parts_ref[...].astype(jnp.float32), axis=0)
    state = (resid_ref[...] + total).astype(jnp.bfloat16)
    head = rows_by_weight(state, head_ref[...])
    here = lax.axis_index("req")
    place = place_ref[...].astype(jnp.float32)
    wanted = jnp.where(here < half, place[0:1], place[1:2])
    eye = lax.broadcasted_iota(jnp.int32, (pairs, pairs), 0) == lax.broadcasted_iota(
        jnp.int32, (pairs, pairs), 1
    )
    column = jnp.sum(
        jnp.where(eye, jnp.broadcast_to(wanted, (pairs, pairs)), 0.0), axis=1, keepdims=True
    )
    base = ((here % half) * rows).astype(jnp.float32)
    picked = jnp.zeros((pairs, head.shape[1]), jnp.float32)
    for r in range(rows):
        picked = jnp.where(column == base + r, jnp.broadcast_to(head[r : r + 1], picked.shape), picked)
    out_ref[...] = picked.reshape(out_ref.shape)


def whole(count, space):
    return [pl.BlockSpec(memory_space=space)] * count


def tp_exchange(parts):
    return lax.all_to_all(parts, "tp", 0, 0)


def on_device(
    inputs,
    gain_attn,
    w_qkv,
    k_cache,
    v_cache,
    lengths,
    pad_mask,
    w_out,
    gain_mlp,
    w_up,
    w_down,
    w_head,
    placement,
    guide,
):
    rows, model = inputs.shape
    width = w_qkv.shape[1]
    peers = lax.axis_size("tp")
    params = pltpu.CompilerParams(vmem_limit_bytes=VMEM_BYTES)
    parts_shape = jax.ShapeDtypeStruct((peers, rows, model), jnp.bfloat16)
    parts = pl.pallas_call(
        attend_kernel,
        out_shape=parts_shape,
        in_specs=whole(8, pl.ANY),
        out_specs=pl.BlockSpec(memory_space=pltpu.VMEM),
        scratch_shapes=[
            pltpu.VMEM(inputs.shape, inputs.dtype),
            pltpu.VMEM((1, model), jnp.float32),
            pltpu.VMEM(w_qkv.shape, w_qkv.dtype),
            pltpu.VMEM(k_cache.shape, k_cache.dtype),
            pltpu.VMEM(v_cache.shape, v_cache.dtype),
            pltpu.SMEM(lengths.shape, lengths.dtype),
            pltpu.VMEM(pad_mask.shape, pad_mask.dtype),
            pltpu.VMEM(w_out.shape, w_out.dtype),
            pltpu.SemaphoreType.DMA((8 + 2 * rows,)),
        ],
        compiler_params=params,
        name="attend",
    )(inputs, gain_attn[None], w_qkv, k_cache, v_cache, lengths, pad_mask, w_out)
    parts, resid = pl.pallas_call(
        mlp_kernel,
        out_shape=(parts_shape, jax.ShapeDtypeStruct((rows, model), jnp.float32)),
        in_specs=whole(5, pltpu.VMEM),
        out_specs=tuple(whole(2, pltpu.VMEM)),
        compiler_params=params,
        name="mlp",
    )(tp_exchange(parts), inputs, gain_mlp[None], w_up, w_down)
    pairs_here = guide.shape[0]
    devices = lax.axis_size("req")
    slots = pl.pallas_call(
        functools.partial(head_kernel, half=devices // 2),
        out_shape=jax.ShapeDtypeStruct((devices, pairs_here, width), jnp.float32),
        in_specs=whole(4, pltpu.VMEM),
        out_specs=pl.BlockSpec(memory_space=pltpu.VMEM),
        compiler_params=params,
        name="head",
    )(tp_exchange(parts), resid, w_head, placement)
    arrived = lax.all_to_all(slots, "req", 0, 0)
    cond = jnp.sum(arrived[: devices // 2], axis=0)
    uncond = jnp.sum(arrived[devices // 2 :], axis=0)
    return uncond + guide[:, None] * (cond - uncond)


def solution(mesh):
    placed = (
        P("req", None),
        P(),
        P(None, "tp", None),
        P("req", "tp", None),
        P("req", "tp", None),
        P("req"),
        P("req", None),
        P("tp", None),
        P(),
        P("tp", None),
        P("tp", None),
        P("tp", None),
        P(),
        P("req"),
    )
    return jax.shard_map(
        on_device, mesh=mesh, in_specs=placed, out_specs=P("req", "tp"), check_vma=False
    )
```

time: 118 us -> 56.8 us (0.48)
  blocking collectives: 95.4 us -> 28.3 us
  Pallas kernels: 0 us -> 8.23 us
  waiting for transfers between devices: 0 us -> 5.69 us
  other arithmetic: 5.9 us -> 0.68 us
  starting transfers between devices: 0 us -> 4.48 us
  matrix products: 4.29 us -> 0 us
  local copies, waits for them, and re-layouts: 10.9 us -> 8.62 us
    psum x2 -> x0, blocking collectives: 49.5 us -> none  [the longest x1 25.9 us: on_device(): resid = xvals + lax.psum(attn_terms, 'tp')]
    all_gather x1 -> x0, blocking collectives: 45.9 us -> none  [on_device(): every_row = lax.all_gather(head, 'req', axis=0, tiled=True)]
    all_to_all x0 -> x2, blocking collectives: none -> 28.3 us  [the longest x1 20.3 us: on_device(): arrived = lax.all_to_all(slots, 'req', 0, 0)]
    dynamic_slice x12 -> x0, local copies, waits for them, and re-layouts: 9.23 us -> none  [the longest x4 4.64 us: value_pass(): lax.dynamic_slice_in_dim(v_cache, start, block, 2)]
    pallas_call x0 -> x3, Pallas kernels: none -> 8.23 us  [the longest x1 7.39 us: on_device(): pl.pallas_call(attend_kernel, out_shape=parts_shape, in_specs=whole(8, pl...]
    unnamed x21 -> x28, local copies, waits for them, and re-layouts: 0.11 us -> 7.91 us
    all_to_all x0 -> x1, waiting for transfers between devices: none -> 5.69 us  [tp_exchange(): return lax.all_to_all(parts, 'tp', 0, 0)]
    all_to_all x0 -> x1, starting transfers between devices: none -> 4.48 us  [tp_exchange(): return lax.all_to_all(parts, 'tp', 0, 0)]
  transfers between devices with their start and end apart: 0 -> 1, of which waited for: 0 -> 1; matrix products, arithmetic and copies ran while one was open for 0% -> 0% of each run, Pallas kernels for 0% -> 0%
where the time goes in v2:
time: 56.8 us; the launch traced here: 56.1 us
  blocking collectives  28.3 us (50%)
  local copies, waits for them, and re-layouts  8.62 us (15%)
  Pallas kernels  8.23 us (14%)
  waiting for transfers between devices  5.69 us (10%)
  starting transfers between devices  4.48 us (8%)
  other arithmetic  0.68 us (1%)
    all_to_all x1, blocking collectives, on_device(): arrived = lax.all_to_all(slots, 'req', 0, 0)  20.3 us
    all_to_all x1, blocking collectives, tp_exchange(): return lax.all_to_all(parts, 'tp', 0, 0)  8.09 us
    unnamed x28, local copies, waits for them, and re-layouts  7.91 us
    pallas_call x1, Pallas kernels, on_device(): pl.pallas_call(attend_kernel, out_shape=parts_shape, in_specs=whole(8, pl...  7.39 us
    all_to_all x1, waiting for transfers between devices, tp_exchange(): return lax.all_to_all(parts, 'tp', 0, 0)  5.69 us
    all_to_all x1, starting transfers between devices, tp_exchange(): return lax.all_to_all(parts, 'tp', 0, 0)  4.48 us
  transfers between devices with their start and end apart: 1, of which 1 were waited for; matrix products, arithmetic and copies ran while one was open for 0% of the time, Pallas kernels for 0%

profile of v2, /device:TPU:2, one launch (start us, length us, event | category | flops | bytes accessed | tf_op | source)
XLA Modules:
  0.0 56.1 jit_solution(336950328254352173)
XLA Ops:
  0.0 0.7 %broadcast_in_dim.7.gain_hbm = f32[1,1280]{1,0:T(1,128)S(1)} reshape(f32[1280]{0:T(1024)} %param.15) | data formatting | bytes 10240 | tf_op jit(solution)/shard_map/broadcast_in_dim | solution.py:212
  0.7 0.0 copy-start
  0.7 1.7 %copy-done = bf16[4,160,2048]{2,1,0:T(8,128)(2,1)S(1)} copy-done((bf16[4,160,2048]{2,1,0:T(8,128)(2,1)S(1)}, bf16[4,160,2048]{2,1,0:T(8,128)(2,1)}, u32[]{:S(2)}) %copy-start) | copy-done | bytes 2621464
  2.4 0.0 copy-start.1
  2.4 1.7 %copy-done.1 = bf16[4,160,2048]{2,1,0:T(8,128)(2,1)S(1)} copy-done((bf16[4,160,2048]{2,1,0:T(8,128)(2,1)S(1)}, bf16[4,160,2048]{2,1,0:T(8,128)(2,1)}, u32[]{:S(2)}) %copy-start.1) | copy-done | bytes 2621464
  4.2 0.0 copy-start.2
  4.2 1.3 %copy-done.2 = bf16[3,160,1280]{2,1,0:T(8,128)(2,1)S(1)} copy-done((bf16[3,160,1280]{2,1,0:T(8,128)(2,1)S(1)}, bf16[3,160,1280]{2,1,0:T(8,128)(2,1)}, u32[]{:S(2)}) %copy-start.2) | copy-done | bytes 1228824
  5.5 0.0 copy-start.3
  5.5 1.0 %copy-done.3 = bf16[160,1280]{1,0:T(8,128)(2,1)S(1)} copy-done((bf16[160,1280]{1,0:T(8,128)(2,1)S(1)}, bf16[160,1280]{1,0:T(8,128)(2,1)}, u32[]{:S(2)}) %copy-start.3) | copy-done | bytes 409624
  6.5 0.0 copy-start.7
  6.5 0.7 %copy-done.7 = bf16[4,1280]{1,0:T(4,128)(2,1)S(1)} copy-done((bf16[4,1280]{1,0:T(4,128)(2,1)S(1)}, bf16[4,1280]{1,0:T(4,128)(2,1)}, u32[]{:S(2)}) %copy-start.7) | copy-done | bytes 10264
  7.2 0.0 copy-start.9
  7.2 0.8 %copy-done.9 = s32[4,2048]{1,0:T(4,128)S(1)} copy-done((s32[4,2048]{1,0:T(4,128)S(1)}, s32[4,2048]{1,0:T(4,128)}, u32[]{:S(2)}) %copy-start.9) | copy-done | bytes 32792
  7.9 0.0 copy-start.11
  7.9 0.7 %copy-done.11 = s32[4]{0:T(128)S(1)} copy-done((s32[4]{0:T(128)S(1)}, s32[4]{0:T(128)}, u32[]{:S(2)}) %copy-start.11) | copy-done | bytes 40
  8.6 0.0 copy-start.12
  8.6 0.0 copy-start.4
  8.6 0.0 copy-start.5
  8.6 0.0 copy-start.8
  8.6 0.0 copy-start.6
  8.6 0.0 copy-start.10
  8.6 0.0 copy-start.13
  8.6 7.4 %attend.1 = bf16[8,4,1280]{2,1,0:T(4,128)(2,1)} custom-call(bf16[4,1280]{1,0:T(4,128)(2,1)S(1)} %copy-done.7, f32[1,1280]{1,0:T(1,128)S(1)} %broadcast_in_dim.7.gain_hbm, bf16[3,160,1280]{2,1,0:T(8,128)(2,1)S(1)} %copy-done.2, bf16[4,160,2048]{2,1,0:T(8,128)(2,1)S(1)} %copy-done, bf16[4,160,2048]{2,1,0:T(8,128)(2,1)S(1)} %copy-done.1, s32[4]{0:T(128)S(1)} %copy-done.11, ...), custom_call_target="tpu_custom_call" | custom-call | tf_op jit(solution)/shard_map/attend/pallas_call | solution.py:194
  16.0 4.5 %all-to-all-start = ((bf16[8,4,1280]{2,1,0:T(4,128)(2,1)}), bf16[8,4,1280]{2,1,0:T(4,128)(2,1)S(1)}, u32[]{:S(2)}, u32[]{:S(2)}) async-start(bf16[8,4,1280]{2,1,0:T(4,128)(2,1)} %attend.1), calls=%async_computation | async-start | bytes 163840 | tf_op jit(solution)/shard_map/all_to_all | solution.py:170
  20.5 0.0 copy-done.12
  20.5 5.7 %all-to-all-done.parts_ref = bf16[8,4,1280]{2,1,0:T(4,128)(2,1)S(1)} async-done(((bf16[8,4,1280]{2,1,0:T(4,128)(2,1)}), bf16[8,4,1280]{2,1,0:T(4,128)(2,1)S(1)}, u32[]{:S(2)}, u32[]{:S(2)}) %all-to-all-start) | async-done | bytes 81952 | tf_op jit(solution)/shard_map/all_to_all | solution.py:170
  26.2 0.0 copy-done.4
  26.2 0.0 copy-done.5
  26.2 0.0 copy-done.8
  26.2 0.6 %mlp.1 = (bf16[8,4,1280]{2,1,0:T(4,128)(2,1)S(1)}, f32[4,1280]{1,0:T(4,128)S(1)}) custom-call(bf16[8,4,1280]{2,1,0:T(4,128)(2,1)S(1)} %all-to-all-done.parts_ref, bf16[4,1280]{1,0:T(4,128)(2,1)S(1)} %copy-done.8, f32[1,1280]{1,0:T(1,128)S(1)} %broadcast_in_dim.8.gain_ref, bf16[160,1280]{1,0:T(8,128)(2,1)S(1)} %copy-done.4, bf16[160,1280]{1,0:T(8,128)(2,1)S(1)} %copy-done.5), custom_call_target="tpu_custom_call" | custom-call | tf_op jit(solution)/shard_map/mlp/pallas_call | solution.py:213
  26.8 8.1 %all_to_all.15.parts_ref = bf16[8,4,1280]{2,1,0:T(4,128)(2,1)S(1)} all-to-all(bf16[8,4,1280]{2,1,0:T(4,128)(2,1)S(1)} %get-tuple-element.7), channel_id=1, replica_groups=mesh['req'=32,'tp'=8] {'tp'}, dimensions={0} | all-to-all | bytes 163840 | tf_op jit(solution)/shard_map/all_to_all | solution.py:170
  34.9 0.0 copy-done.6
  34.9 0.0 copy-done.10
  34.9 0.3 head.1
  35.2 20.3 %all_to_all.16 = f32[32,2,160]{2,1,0:T(2,128)S(1)} all-to-all(f32[32,2,160]{2,1,0:T(2,128)S(1)} %head.1), channel_id=1, replica_groups=mesh['req'=32,'tp'=8] {'req'}, dimensions={0} | all-to-all | bytes 81920 | tf_op jit(solution)/shard_map/all_to_all | solution.py:231
  55.5 0.0 copy-done.13
  55.5 0.6 %multiply_add_fusion = f32[2,160]{1,0:T(2,128)} fusion(f32[2,160]{1,0:T(2,128)S(1)} %get-tuple-element.10, f32[2,160]{1,0:T(2,128)S(1)} %get-tuple-element.9, f32[2]{0:T(128)S(1)} %copy-done.13), kind=kLoop, calls=%fused_computation.2 | loop fusion | flops 960 | bytes 3848 | tf_op jit(solution)/shard_map/add | solution.py:234
  (2 shorter events, 0.0 us)
Async XLA Ops:
  0.7 1.7 %copy-start = (bf16[4,160,2048]{2,1,0:T(8,128)(2,1)S(1)}, bf16[4,160,2048]{2,1,0:T(8,128)(2,1)}, u32[]{:S(2)}) copy-start(bf16[4,160,2048]{2,1,0:T(8,128)(2,1)} %k_hbm.1) | copy-start | bytes 7864324
  2.4 1.7 %copy-start.1 = (bf16[4,160,2048]{2,1,0:T(8,128)(2,1)S(1)}, bf16[4,160,2048]{2,1,0:T(8,128)(2,1)}, u32[]{:S(2)}) copy-start(bf16[4,160,2048]{2,1,0:T(8,128)(2,1)} %v_hbm.1) | copy-start | bytes 7864324
  4.2 1.3 %copy-start.2 = (bf16[3,160,1280]{2,1,0:T(8,128)(2,1)S(1)}, bf16[3,160,1280]{2,1,0:T(8,128)(2,1)}, u32[]{:S(2)}) copy-start(bf16[3,160,1280]{2,1,0:T(8,128)(2,1)} %w_hbm.1) | copy-start | bytes 3686404
  5.5 1.0 %copy-start.3 = (bf16[160,1280]{1,0:T(8,128)(2,1)S(1)}, bf16[160,1280]{1,0:T(8,128)(2,1)}, u32[]{:S(2)}) copy-start(bf16[160,1280]{1,0:T(8,128)(2,1)} %wo_hbm.1) | copy-start | bytes 1228804
  6.5 0.7 %copy-start.7 = (bf16[4,1280]{1,0:T(4,128)(2,1)S(1)}, bf16[4,1280]{1,0:T(4,128)(2,1)}, u32[]{:S(2)}) copy-start(bf16[4,1280]{1,0:T(4,128)(2,1)} %x_ref.1) | copy-start | bytes 30724
  7.2 0.8 %copy-start.9 = (s32[4,2048]{1,0:T(4,128)S(1)}, s32[4,2048]{1,0:T(4,128)}, u32[]{:S(2)}) copy-start(s32[4,2048]{1,0:T(4,128)} %pad_hbm.1) | copy-start | bytes 98308
  7.9 0.7 %copy-start.11 = (s32[4]{0:T(128)S(1)}, s32[4]{0:T(128)}, u32[]{:S(2)}) copy-start(s32[4]{0:T(128)} %len_hbm.1) | copy-start | bytes 52
  8.6 11.9 %copy-start.12 = (f32[1280]{0:T(1024)S(1)}, f32[1280]{0:T(1024)}, u32[]{:S(2)}) copy-start(f32[1280]{0:T(1024)} %param.22) | copy-start | bytes 15364
  8.6 17.6 %copy-start.4 = (bf16[160,1280]{1,0:T(8,128)(2,1)S(1)}, bf16[160,1280]{1,0:T(8,128)(2,1)}, u32[]{:S(2)}) copy-start(bf16[160,1280]{1,0:T(8,128)(2,1)} %up_ref.1) | copy-start | bytes 1228804
  8.6 17.6 %copy-start.5 = (bf16[160,1280]{1,0:T(8,128)(2,1)S(1)}, bf16[160,1280]{1,0:T(8,128)(2,1)}, u32[]{:S(2)}) copy-start(bf16[160,1280]{1,0:T(8,128)(2,1)} %down_ref.1) | copy-start | bytes 1228804
  8.6 17.6 %copy-start.8 = (bf16[4,1280]{1,0:T(4,128)(2,1)S(1)}, bf16[4,1280]{1,0:T(4,128)(2,1)}, u32[]{:S(2)}) copy-start(bf16[4,1280]{1,0:T(4,128)(2,1)} %x_ref.1) | copy-start | bytes 30724
  8.6 26.3 %copy-start.6 = (bf16[160,1280]{1,0:T(8,128)(2,1)S(1)}, bf16[160,1280]{1,0:T(8,128)(2,1)}, u32[]{:S(2)}) copy-start(bf16[160,1280]{1,0:T(8,128)(2,1)} %head_ref.1) | copy-start | bytes 1228804
  8.6 26.3 %copy-start.10 = (s32[2,64]{1,0:T(2,128)S(1)}, s32[2,64]{1,0:T(2,128)}, u32[]{:S(2)}) copy-start(s32[2,64]{1,0:T(2,128)} %place_ref.1) | copy-start | bytes 1540
  8.6 46.8 %copy-start.13 = (f32[2]{0:T(128)S(1)}, f32[2]{0:T(128)}, u32[]{:S(2)}) copy-start(f32[2]{0:T(128)} %param.27) | copy-start | bytes 28
  16.0 10.2 %all-to-all-start = ((bf16[8,4,1280]{2,1,0:T(4,128)(2,1)}), bf16[8,4,1280]{2,1,0:T(4,128)(2,1)S(1)}, u32[]{:S(2)}, u32[]{:S(2)}) async-start(bf16[8,4,1280]{2,1,0:T(4,128)(2,1)} %attend.1), calls=%async_computation | async-start | bytes 163840 | tf_op jit(solution)/shard_map/all_to_all | solution.py:170

commit v3 on v2

--- a/solution.py
+++ b/solution.py
@@ -79,7 +79,7 @@
     own_head = col_n // HEAD_DIM == row_n % heads
     x_in.wait()
     gain_in.wait()
-    normed = rms_gain(x_v[...].astype(jnp.float32), gain_v[...]).astype(jnp.bfloat16)
+    normed = rms_gain(x_v[...].astype(jnp.float32), gain_v[...][None]).astype(jnp.bfloat16)
 
     len_in.wait()
     pad_in.wait()
@@ -132,7 +132,7 @@
 def mlp_kernel(parts_ref, x_ref, gain_ref, up_ref, down_ref, out_ref, resid_ref):
     resid = x_ref[...].astype(jnp.float32) + jnp.sum(parts_ref[...].astype(jnp.float32), axis=0)
     resid_ref[...] = resid
-    normed = rms_gain(resid, gain_ref[...]).astype(jnp.bfloat16)
+    normed = rms_gain(resid, gain_ref[...][None]).astype(jnp.bfloat16)
     hidden = jax.nn.gelu(rows_by_weight(normed, up_ref[...]), approximate=True)
     terms = jnp.dot(hidden.astype(jnp.bfloat16), down_ref[...], preferred_element_type=jnp.float32)
     terms = terms.astype(out_ref.dtype)
@@ -194,11 +194,11 @@
     parts = pl.pallas_call(
         attend_kernel,
         out_shape=parts_shape,
-        in_specs=whole(8, pl.ANY),
+        in_specs=whole(8, pltpu.HBM),
         out_specs=pl.BlockSpec(memory_space=pltpu.VMEM),
         scratch_shapes=[
             pltpu.VMEM(inputs.shape, inputs.dtype),
-            pltpu.VMEM((1, model), jnp.float32),
+            pltpu.VMEM((model,), jnp.float32),
             pltpu.VMEM(w_qkv.shape, w_qkv.dtype),
             pltpu.VMEM(k_cache.shape, k_cache.dtype),
             pltpu.VMEM(v_cache.shape, v_cache.dtype),
@@ -209,7 +209,7 @@
         ],
         compiler_params=params,
         name="attend",
-    )(inputs, gain_attn[None], w_qkv, k_cache, v_cache, lengths, pad_mask, w_out)
+    )(*[pltpu.with_memory_space_constraint(a, pltpu.HBM) for a in (inputs, gain_attn, w_qkv, k_cache, v_cache, lengths, pad_mask, w_out)])
     parts, resid = pl.pallas_call(
         mlp_kernel,
         out_shape=(parts_shape, jax.ShapeDtypeStruct((rows, model), jnp.float32)),
@@ -217,7 +217,7 @@
         out_specs=tuple(whole(2, pltpu.VMEM)),
         compiler_params=params,
         name="mlp",
-    )(tp_exchange(parts), inputs, gain_mlp[None], w_up, w_down)
+    )(tp_exchange(parts), inputs, gain_mlp, w_up, w_down)
     pairs_here = guide.shape[0]
     devices = lax.axis_size("req")
     slots = pl.pallas_call(

time: 56.8 us -> 45.5 us (0.80)
  blocking collectives: 28.3 us -> 38.3 us
  local copies, waits for them, and re-layouts: 8.62 us -> 0.03 us
  waiting for transfers between devices: 5.69 us -> 0 us
  starting transfers between devices: 4.48 us -> 0 us
  Pallas kernels: 8.23 us -> 6.1 us
    all_to_all x1 -> x2, blocking collectives: 8.09 us -> 18.1 us  [tp_exchange(): return lax.all_to_all(parts, 'tp', 0, 0)]
    unnamed x28 -> x14, local copies, waits for them, and re-layouts: 7.91 us -> 0.03 us
    all_to_all x1 -> x0, waiting for transfers between devices: 5.69 us -> none  [tp_exchange(): return lax.all_to_all(parts, 'tp', 0, 0)]
    all_to_all x1 -> x0, starting transfers between devices: 4.48 us -> none  [tp_exchange(): return lax.all_to_all(parts, 'tp', 0, 0)]
    pallas_call x1, Pallas kernels: 7.39 us -> 5.26 us  [on_device(): pl.pallas_call(attend_kernel, out_shape=parts_shape, in_specs=whole(8, pl...]
    broadcast_in_dim x2 -> x0, local copies, waits for them, and re-layouts: 0.71 us -> none  [the longest x1 0.7 us: on_device(): gain_attn[None]]
  transfers between devices with their start and end apart: 1 -> 0, of which waited for: 1 -> 0; matrix products, arithmetic and copies ran while one was open for 0% -> 0% of each run, Pallas kernels for 0% -> 0%
where the time goes in v3:
time: 45.5 us; the launch traced here: 45.2 us
  blocking collectives  38.3 us (84%)
  Pallas kernels  6.1 us (13%)
  other arithmetic  0.68 us (1%)
    all_to_all x1, blocking collectives, on_device(): arrived = lax.all_to_all(slots, 'req', 0, 0)  20.3 us
    all_to_all x2, blocking collectives, tp_exchange(): return lax.all_to_all(parts, 'tp', 0, 0)  18.1 us
    pallas_call x1, Pallas kernels, on_device(): pl.pallas_call(attend_kernel, out_shape=parts_shape, in_specs=whole(8, pl...  5.26 us

profile of v3, /device:TPU:2, one launch (start us, length us, event | category | flops | bytes accessed | tf_op | source)
XLA Modules:
  0.0 45.2 jit_solution(6759325354318321200)
XLA Ops:
  0.0 0.0 copy-start.3
  0.0 0.0 copy-start.1
  0.0 0.0 copy-start
  0.0 0.0 copy-start.4
  0.0 0.0 copy-start.5
  0.0 0.0 copy-start.2
  0.0 0.0 copy-start.6
  0.0 5.3 %attend.1 = bf16[8,4,1280]{2,1,0:T(4,128)(2,1)S(1)} custom-call(bf16[4,1280]{1,0:T(4,128)(2,1)} %x_ref.1, f32[1280]{0:T(1024)} %gain_hbm.1, bf16[3,160,1280]{2,1,0:T(8,128)(2,1)} %w_hbm.1, bf16[4,160,2048]{2,1,0:T(8,128)(2,1)} %k_hbm.1, bf16[4,160,2048]{2,1,0:T(8,128)(2,1)} %v_hbm.1, s32[4]{0:T(128)} %len_hbm.1, s32[4,2048]{1,0:T(4,128)} %pad_hbm.1, ...), custom_call_target="tpu_custom_call" | custom-call | tf_op jit(solution)/shard_map/attend/pallas_call | solution.py:194
  5.3 10.0 %all_to_all.15.parts_ref = bf16[8,4,1280]{2,1,0:T(4,128)(2,1)S(1)} all-to-all(bf16[8,4,1280]{2,1,0:T(4,128)(2,1)S(1)} %attend.1), channel_id=1, replica_groups=mesh['req'=32,'tp'=8] {'tp'}, dimensions={0} | all-to-all | bytes 163840 | tf_op jit(solution)/shard_map/all_to_all | solution.py:170
  15.3 0.0 copy-done.3
  15.3 0.0 copy-done.1
  15.3 0.0 copy-done
  15.3 0.0 copy-done.4
  15.3 0.6 %mlp.1 = (bf16[8,4,1280]{2,1,0:T(4,128)(2,1)S(1)}, f32[4,1280]{1,0:T(4,128)S(1)}) custom-call(bf16[8,4,1280]{2,1,0:T(4,128)(2,1)S(1)} %all_to_all.15.parts_ref, bf16[4,1280]{1,0:T(4,128)(2,1)S(1)} %copy-done.3, f32[1280]{0:T(1024)S(1)} %copy-done.4, bf16[160,1280]{1,0:T(8,128)(2,1)S(1)} %copy-done, bf16[160,1280]{1,0:T(8,128)(2,1)S(1)} %copy-done.1), custom_call_target="tpu_custom_call" | custom-call | tf_op jit(solution)/shard_map/mlp/pallas_call | solution.py:213
  15.9 8.1 %all_to_all.16.parts_ref = bf16[8,4,1280]{2,1,0:T(4,128)(2,1)S(1)} all-to-all(bf16[8,4,1280]{2,1,0:T(4,128)(2,1)S(1)} %get-tuple-element.7), channel_id=1, replica_groups=mesh['req'=32,'tp'=8] {'tp'}, dimensions={0} | all-to-all | bytes 163840 | tf_op jit(solution)/shard_map/all_to_all | solution.py:170
  24.0 0.0 copy-done.5
  24.0 0.0 copy-done.2
  24.0 0.3 head.1
  24.3 20.3 %all_to_all.17 = f32[32,2,160]{2,1,0:T(2,128)S(1)} all-to-all(f32[32,2,160]{2,1,0:T(2,128)S(1)} %head.1), channel_id=1, replica_groups=mesh['req'=32,'tp'=8] {'req'}, dimensions={0} | all-to-all | bytes 81920 | tf_op jit(solution)/shard_map/all_to_all | solution.py:231
  44.6 0.0 copy-done.6
  44.6 0.6 %multiply_add_fusion = f32[2,160]{1,0:T(2,128)} fusion(f32[2,160]{1,0:T(2,128)S(1)} %get-tuple-element.10, f32[2,160]{1,0:T(2,128)S(1)} %get-tuple-element.9, f32[2]{0:T(128)S(1)} %copy-done.6), kind=kLoop, calls=%fused_computation.2 | loop fusion | flops 960 | bytes 3848 | tf_op jit(solution)/shard_map/add | solution.py:234
  (1 shorter events, 0.0 us)
Async XLA Ops:
  0.0 15.3 %copy-start.3 = (bf16[4,1280]{1,0:T(4,128)(2,1)S(1)}, bf16[4,1280]{1,0:T(4,128)(2,1)}, u32[]{:S(2)}) copy-start(bf16[4,1280]{1,0:T(4,128)(2,1)} %x_ref.1) | copy-start | bytes 30724
  0.0 15.3 %copy-start.1 = (bf16[160,1280]{1,0:T(8,128)(2,1)S(1)}, bf16[160,1280]{1,0:T(8,128)(2,1)}, u32[]{:S(2)}) copy-start(bf16[160,1280]{1,0:T(8,128)(2,1)} %down_ref.1) | copy-start | bytes 1228804
  0.0 15.3 %copy-start = (bf16[160,1280]{1,0:T(8,128)(2,1)S(1)}, bf16[160,1280]{1,0:T(8,128)(2,1)}, u32[]{:S(2)}) copy-start(bf16[160,1280]{1,0:T(8,128)(2,1)} %up_ref.1) | copy-start | bytes 1228804
  0.0 15.3 %copy-start.4 = (f32[1280]{0:T(1024)S(1)}, f32[1280]{0:T(1024)}, u32[]{:S(2)}) copy-start(f32[1280]{0:T(1024)} %gain_ref.1) | copy-start | bytes 15364
  0.0 24.0 %copy-start.5 = (s32[2,64]{1,0:T(2,128)S(1)}, s32[2,64]{1,0:T(2,128)}, u32[]{:S(2)}) copy-start(s32[2,64]{1,0:T(2,128)} %place_ref.1) | copy-start | bytes 1540
  0.0 24.0 %copy-start.2 = (bf16[160,1280]{1,0:T(8,128)(2,1)S(1)}, bf16[160,1280]{1,0:T(8,128)(2,1)}, u32[]{:S(2)}) copy-start(bf16[160,1280]{1,0:T(8,128)(2,1)} %head_ref.1) | copy-start | bytes 1228804
  0.0 44.5 %copy-start.6 = (f32[2]{0:T(128)S(1)}, f32[2]{0:T(128)}, u32[]{:S(2)}) copy-start(f32[2]{0:T(128)} %param.27) | copy-start | bytes 28

commit v4 on v3

--- a/solution.py
+++ b/solution.py
@@ -9,6 +9,8 @@
 
 HEAD_DIM = 80
 NEG = -1e30
+LANES = 128
+BATCHES = 2
 VMEM_BYTES = 40 << 20
 
 
@@ -52,79 +54,87 @@
     rows, width, slots = k_v.shape
     heads = width // HEAD_DIM
     many = rows * heads
+    group = rows // BATCHES
     copies = [
         (x_hbm, x_v),
         (gain_hbm, gain_v),
-        (w_hbm.at[0], w_v.at[0]),
         (len_hbm, len_s),
         (pad_hbm, pad_v),
+        (w_hbm, w_v),
     ]
-    copies += [(k_hbm.at[r], k_v.at[r]) for r in range(rows)]
-    copies += [(w_hbm.at[1], w_v.at[1]), (w_hbm.at[2], w_v.at[2])]
-    copies += [(v_hbm.at[r], v_v.at[r]) for r in range(rows)]
-    copies += [(wo_hbm, wo_v)]
+    for a, b in ((k_hbm, k_v), (v_hbm, v_v)):
+        for i in range(BATCHES):
+            part = pl.ds(i * group, group)
+            copies.append((a.at[part], b.at[part]))
+    copies.append((wo_hbm, wo_v))
     flights = [pltpu.make_async_copy(a, b, sems.at[i]) for i, (a, b) in enumerate(copies)]
     for flight in flights:
         flight.start()
-    x_in, gain_in, wq_in, len_in, pad_in = flights[:5]
-    k_in = flights[5 : 5 + rows]
-    wk_in, wv_in = flights[5 + rows : 7 + rows]
-    v_in = flights[7 + rows : 7 + 2 * rows]
-    wo_in = flights[7 + 2 * rows]
+    w_in = flights[4]
+    k_in = flights[5 : 5 + BATCHES]
+    v_in = flights[5 + BATCHES : 5 + 2 * BATCHES]
+    wo_in = flights[5 + 2 * BATCHES]
     scale = HEAD_DIM ** (-0.5)
 
-    row_n = lax.broadcasted_iota(jnp.int32, (many, width), 0)
-    col_n = lax.broadcasted_iota(jnp.int32, (many, width), 1)
-    owner_n = row_n // heads
-    own_head = col_n // HEAD_DIM == row_n % heads
-    x_in.wait()
-    gain_in.wait()
+    owner = lax.broadcasted_iota(jnp.int32, (many, width), 0) // heads
+    which = lax.broadcasted_iota(jnp.int32, (many, width), 0) % heads
+    own_head = lax.broadcasted_iota(jnp.int32, (many, width), 1) // HEAD_DIM == which
+    for flight in flights[:4]:
+        flight.wait()
     normed = rms_gain(x_v[...].astype(jnp.float32), gain_v[...][None]).astype(jnp.bfloat16)
-
-    len_in.wait()
-    pad_in.wait()
-    row_w = lax.broadcasted_iota(jnp.int32, (many, slots), 0) // heads
-    col_w = lax.broadcasted_iota(jnp.int32, (many, slots), 1)
+    owner_slot = lax.broadcasted_iota(jnp.int32, (many, slots), 0) // heads
     filled = jnp.full((many, slots), len_s[0], jnp.int32)
     for r in range(1, rows):
-        filled = jnp.where(row_w == r, len_s[r], filled)
-    valid = (col_w < filled) & (spread(pad_v[...], row_w, rows) == 1)
-
-    def project(which):
-        flat = rows_by_weight(normed, w_v[which])
-        return spread(flat.astype(jnp.bfloat16).astype(jnp.float32), owner_n, rows)
-
-    wq_in.wait()
-    query = jnp.where(own_head, project(0), 0.0)
+        filled = jnp.where(owner_slot == r, len_s[r], filled)
+    valid = lax.broadcasted_iota(jnp.int32, (many, slots), 1) < filled
+    valid = valid & (spread(pad_v[...], owner_slot, rows) == 1)
+
+    w_in.wait()
+    fused = rows_by_weight(normed, w_v[...]).astype(jnp.bfloat16).astype(jnp.float32)
+    fused = spread(fused, lax.broadcasted_iota(jnp.int32, (many, 3 * width), 0) // heads, rows)
+    query = jnp.where(own_head, fused[:, :width], 0.0)
+    key_new = fused[:, width : 2 * width]
+    value_new = fused[:, 2 * width :]
+    own = jnp.sum(query * key_new, axis=1, keepdims=True) * scale
     scores = None
     for r in range(rows):
-        picked = jnp.where(owner_n == r, query, 0.0).astype(jnp.bfloat16)
-        k_in[r].wait()
+        if r % group == 0:
+            k_in[r // group].wait()
+        picked = jnp.where(owner == r, query, 0.0).astype(jnp.bfloat16)
         part = jnp.dot(picked, k_v[r], preferred_element_type=jnp.float32)
         scores = part if scores is None else scores + part
     scores = jnp.where(valid, scores * scale, NEG)
-    wk_in.wait()
-    own = jnp.sum(query * project(1), axis=1, keepdims=True) * scale
-    wv_in.wait()
-    value_new = project(2)
     top = jnp.maximum(jnp.max(scores, axis=1, keepdims=True), own)
     expo = jnp.where(valid, jnp.exp(scores - top), 0.0)
     own_exp = jnp.exp(own - top)
-    total = jnp.sum(expo, axis=1, keepdims=True) + own_exp
-    probs = (expo / total).astype(jnp.bfloat16)
-    own_prob = (own_exp / total).astype(jnp.bfloat16).astype(jnp.float32)
-    mixed = own_prob * value_new
+    inverse = 1.0 / (jnp.sum(expo, axis=1, keepdims=True) + own_exp)
+    probs = (expo * inverse).astype(jnp.bfloat16).astype(jnp.float32)
+    own_prob = (own_exp * inverse).astype(jnp.bfloat16).astype(jnp.float32)
+    fresh = jnp.where(own_head, own_prob * value_new, 0.0)
+    mixed = fresh
+    for h in range(1, heads):
+        mixed = mixed + pltpu.roll(fresh, many - h, 0)
+    mixed = jnp.concatenate([mixed[r * heads : r * heads + 1] for r in range(rows)], axis=0)
+
+    lane = lax.broadcasted_iota(jnp.int32, (width, LANES), 1)
+    columns = jnp.zeros((width, LANES), jnp.float32)
     for r in range(rows):
-        v_in[r].wait()
-        mixed = mixed + jnp.where(owner_n == r, rows_by_weight(probs, v_v[r]), 0.0)
-    mixed = jnp.where(own_head, mixed, 0.0).astype(jnp.bfloat16).astype(jnp.float32)
-    attn = mixed
-    for h in range(1, heads):
-        attn = attn + pltpu.roll(mixed, many - h, 0)
+        if r % group == 0:
+            v_in[r // group].wait()
+        sums = []
+        for h in range(heads):
+            weights = probs[r * heads + h : r * heads + h + 1]
+            acc = None
+            for c in range(0, slots, LANES):
+                block = v_v[r, pl.ds(h * HEAD_DIM, HEAD_DIM), pl.ds(c, LANES)].astype(jnp.float32)
+                block = block * weights[:, c : c + LANES]
+                acc = block if acc is None else acc + block
+            sums.append(acc)
+        column = jnp.sum(jnp.concatenate(sums, axis=0), axis=1, keepdims=True)
+        columns = jnp.where(lane == r, column, columns)
+    attn = (mixed + columns.T[:rows]).astype(jnp.bfloat16)
     wo_in.wait()
-    terms = jnp.dot(attn.astype(jnp.bfloat16), wo_v[...], preferred_element_type=jnp.float32)
-    terms = jnp.concatenate([terms[r * heads : r * heads + 1] for r in range(rows)], axis=0)
-    terms = terms.astype(out_ref.dtype)
+    terms = jnp.dot(attn, wo_v[...], preferred_element_type=jnp.float32).astype(out_ref.dtype)
     for t in range(out_ref.shape[0]):
         out_ref[t] = terms
 
@@ -132,8 +142,9 @@
 def mlp_kernel(parts_ref, x_ref, gain_ref, up_ref, down_ref, out_ref, resid_ref):
     resid = x_ref[...].astype(jnp.float32) + jnp.sum(parts_ref[...].astype(jnp.float32), axis=0)
     resid_ref[...] = resid
-    normed = rms_gain(resid, gain_ref[...][None]).astype(jnp.bfloat16)
-    hidden = jax.nn.gelu(rows_by_weight(normed, up_ref[...]), approximate=True)
+    inverse = lax.rsqrt(jnp.mean(resid * resid, axis=-1, keepdims=True) + 1e-06)
+    scaled = (resid * gain_ref[...][None]).astype(jnp.bfloat16)
+    hidden = jax.nn.gelu(rows_by_weight(scaled, up_ref[...]) * inverse, approximate=True)
     terms = jnp.dot(hidden.astype(jnp.bfloat16), down_ref[...], preferred_element_type=jnp.float32)
     terms = terms.astype(out_ref.dtype)
     for t in range(out_ref.shape[0]):
@@ -191,6 +202,8 @@
     peers = lax.axis_size("tp")
     params = pltpu.CompilerParams(vmem_limit_bytes=VMEM_BYTES)
     parts_shape = jax.ShapeDtypeStruct((peers, rows, model), jnp.bfloat16)
+    fused = w_qkv.reshape(-1, model)
+    operands = (inputs, gain_attn, fused, k_cache, v_cache, lengths, pad_mask, w_out)
     parts = pl.pallas_call(
         attend_kernel,
         out_shape=parts_shape,
@@ -199,17 +212,17 @@
         scratch_shapes=[
             pltpu.VMEM(inputs.shape, inputs.dtype),
             pltpu.VMEM((model,), jnp.float32),
-            pltpu.VMEM(w_qkv.shape, w_qkv.dtype),
+            pltpu.VMEM(fused.shape, fused.dtype),
             pltpu.VMEM(k_cache.shape, k_cache.dtype),
             pltpu.VMEM(v_cache.shape, v_cache.dtype),
             pltpu.SMEM(lengths.shape, lengths.dtype),
             pltpu.VMEM(pad_mask.shape, pad_mask.dtype),
             pltpu.VMEM(w_out.shape, w_out.dtype),
-            pltpu.SemaphoreType.DMA((8 + 2 * rows,)),
+            pltpu.SemaphoreType.DMA((6 + 2 * BATCHES,)),
         ],
         compiler_params=params,
         name="attend",
-    )(*[pltpu.with_memory_space_constraint(a, pltpu.HBM) for a in (inputs, gain_attn, w_qkv, k_cache, v_cache, lengths, pad_mask, w_out)])
+    )(*(pltpu.with_memory_space_constraint(a, pltpu.HBM) for a in operands))
     parts, resid = pl.pallas_call(
         mlp_kernel,
         out_shape=(parts_shape, jax.ShapeDtypeStruct((rows, model), jnp.float32)),

time: 45.5 us -> 44.1 us (0.969)
  Pallas kernels: 6.1 us -> 4.62 us
    pallas_call x1, Pallas kernels: 5.26 us -> 3.87 us  [on_device(): pl.pallas_call(attend_kernel, out_shape=parts_shape, in_specs=whole(8, pl...]
where the time goes in v4:
time: 44.1 us; the launch traced here: 43.7 us
  blocking collectives  38.3 us (87%)
  Pallas kernels  4.62 us (10%)
  other arithmetic  0.68 us (2%)
    all_to_all x1, blocking collectives, on_device(): arrived = lax.all_to_all(slots, 'req', 0, 0)  20.3 us
    all_to_all x2, blocking collectives, tp_exchange(): return lax.all_to_all(parts, 'tp', 0, 0)  18.1 us
    pallas_call x1, Pallas kernels, on_device(): pl.pallas_call(attend_kernel, out_shape=parts_shape, in_specs=whole(8, pl...  3.87 us

profile of v4, /device:TPU:2, one launch (start us, length us, event | category | flops | bytes accessed | tf_op | source)
XLA Modules:
  0.0 43.7 jit_solution(13144040527643037734)
XLA Ops:
  0.0 0.0 copy-start
  0.0 0.0 copy-start.1
  0.0 0.0 copy-start.3
  0.0 0.0 copy-start.4
  0.0 0.0 copy-start.2
  0.0 0.0 copy-start.5
  0.0 0.0 copy-start.6
  0.0 3.9 %attend.1 = bf16[8,4,1280]{2,1,0:T(4,128)(2,1)S(1)} custom-call(bf16[4,1280]{1,0:T(4,128)(2,1)} %x_ref.1, f32[1280]{0:T(1024)} %gain_hbm.1, bf16[480,1280]{1,0:T(8,128)(2,1)} %bitcast.1, bf16[4,160,2048]{2,1,0:T(8,128)(2,1)} %k_hbm.1, bf16[4,160,2048]{2,1,0:T(8,128)(2,1)} %v_hbm.1, s32[4]{0:T(128)} %len_hbm.1, s32[4,2048]{1,0:T(4,128)} %pad_hbm.1, ...), custom_call_target="tpu_custom_call" | custom-call | tf_op jit(solution)/shard_map/attend/pallas_call | solution.py:207
  3.9 10.0 %all_to_all.15.parts_ref = bf16[8,4,1280]{2,1,0:T(4,128)(2,1)S(1)} all-to-all(bf16[8,4,1280]{2,1,0:T(4,128)(2,1)S(1)} %attend.1), channel_id=1, replica_groups=mesh['req'=32,'tp'=8] {'tp'}, dimensions={0} | all-to-all | bytes 163840 | tf_op jit(solution)/shard_map/all_to_all | solution.py:181
  13.9 0.0 copy-done
  13.9 0.0 copy-done.1
  13.9 0.0 copy-done.3
  13.9 0.0 copy-done.4
  13.9 0.5 %mlp.1 = (bf16[8,4,1280]{2,1,0:T(4,128)(2,1)S(1)}, f32[4,1280]{1,0:T(4,128)S(1)}) custom-call(bf16[8,4,1280]{2,1,0:T(4,128)(2,1)S(1)} %all_to_all.15.parts_ref, bf16[4,1280]{1,0:T(4,128)(2,1)S(1)} %copy-done.3, f32[1280]{0:T(1024)S(1)} %copy-done.4, bf16[160,1280]{1,0:T(8,128)(2,1)S(1)} %copy-done, bf16[160,1280]{1,0:T(8,128)(2,1)S(1)} %copy-done.1), custom_call_target="tpu_custom_call" | custom-call | tf_op jit(solution)/shard_map/mlp/pallas_call | solution.py:226
  14.4 8.1 %all_to_all.16.parts_ref = bf16[8,4,1280]{2,1,0:T(4,128)(2,1)S(1)} all-to-all(bf16[8,4,1280]{2,1,0:T(4,128)(2,1)S(1)} %get-tuple-element.7), channel_id=1, replica_groups=mesh['req'=32,'tp'=8] {'tp'}, dimensions={0} | all-to-all | bytes 163840 | tf_op jit(solution)/shard_map/all_to_all | solution.py:181
  22.5 0.0 copy-done.2
  22.5 0.0 copy-done.5
  22.5 0.3 head.1
  22.8 20.3 %all_to_all.17 = f32[32,2,160]{2,1,0:T(2,128)S(1)} all-to-all(f32[32,2,160]{2,1,0:T(2,128)S(1)} %head.1), channel_id=1, replica_groups=mesh['req'=32,'tp'=8] {'req'}, dimensions={0} | all-to-all | bytes 81920 | tf_op jit(solution)/shard_map/all_to_all | solution.py:244
  43.1 0.0 copy-done.6
  43.1 0.6 %multiply_add_fusion = f32[2,160]{1,0:T(2,128)} fusion(f32[2,160]{1,0:T(2,128)S(1)} %get-tuple-element.10, f32[2,160]{1,0:T(2,128)S(1)} %get-tuple-element.9, f32[2]{0:T(128)S(1)} %copy-done.6), kind=kLoop, calls=%fused_computation.2 | loop fusion | flops 960 | bytes 3848 | tf_op jit(solution)/shard_map/add | solution.py:247
  (1 shorter events, 0.0 us)
Async XLA Ops:
  0.0 13.9 %copy-start = (bf16[160,1280]{1,0:T(8,128)(2,1)S(1)}, bf16[160,1280]{1,0:T(8,128)(2,1)}, u32[]{:S(2)}) copy-start(bf16[160,1280]{1,0:T(8,128)(2,1)} %up_ref.1) | copy-start | bytes 1228804
  0.0 13.9 %copy-start.1 = (bf16[160,1280]{1,0:T(8,128)(2,1)S(1)}, bf16[160,1280]{1,0:T(8,128)(2,1)}, u32[]{:S(2)}) copy-start(bf16[160,1280]{1,0:T(8,128)(2,1)} %down_ref.1) | copy-start | bytes 1228804
  0.0 13.9 %copy-start.3 = (bf16[4,1280]{1,0:T(4,128)(2,1)S(1)}, bf16[4,1280]{1,0:T(4,128)(2,1)}, u32[]{:S(2)}) copy-start(bf16[4,1280]{1,0:T(4,128)(2,1)} %x_ref.1) | copy-start | bytes 30724
  0.0 13.9 %copy-start.4 = (f32[1280]{0:T(1024)S(1)}, f32[1280]{0:T(1024)}, u32[]{:S(2)}) copy-start(f32[1280]{0:T(1024)} %gain_ref.1) | copy-start | bytes 15364
  0.0 22.5 %copy-start.2 = (bf16[160,1280]{1,0:T(8,128)(2,1)S(1)}, bf16[160,1280]{1,0:T(8,128)(2,1)}, u32[]{:S(2)}) copy-start(bf16[160,1280]{1,0:T(8,128)(2,1)} %head_ref.1) | copy-start | bytes 1228804
  0.0 22.5 %copy-start.5 = (s32[2,64]{1,0:T(2,128)S(1)}, s32[2,64]{1,0:T(2,128)}, u32[]{:S(2)}) copy-start(s32[2,64]{1,0:T(2,128)} %place_ref.1) | copy-start | bytes 1540
  0.0 43.0 %copy-start.6 = (f32[2]{0:T(128)S(1)}, f32[2]{0:T(128)}, u32[]{:S(2)}) copy-start(f32[2]{0:T(128)} %param.27) | copy-start | bytes 28

commit v5 on v4

--- a/solution.py
+++ b/solution.py
@@ -173,6 +173,20 @@
     out_ref[...] = picked.reshape(out_ref.shape)
 
 
+def guide_kernel(arrived_ref, guide_ref, out_ref, value_v, sem, *, half):
+    cond = jnp.sum(arrived_ref[:half], axis=0)
+    uncond = jnp.sum(arrived_ref[half:], axis=0)
+    weights = guide_ref[...][None]
+    row = lax.broadcasted_iota(jnp.int32, cond.shape, 0)
+    weight = jnp.broadcast_to(weights[:, 0:1], cond.shape)
+    for j in range(1, cond.shape[0]):
+        weight = jnp.where(row == j, jnp.broadcast_to(weights[:, j : j + 1], cond.shape), weight)
+    value_v[...] = uncond + weight * (cond - uncond)
+    copy = pltpu.make_async_copy(value_v, out_ref, sem)
+    copy.start()
+    copy.wait()
+
+
 def whole(count, space):
     return [pl.BlockSpec(memory_space=space)] * count
 
@@ -242,9 +256,18 @@
         name="head",
     )(tp_exchange(parts), resid, w_head, placement)
     arrived = lax.all_to_all(slots, "req", 0, 0)
-    cond = jnp.sum(arrived[: devices // 2], axis=0)
-    uncond = jnp.sum(arrived[devices // 2 :], axis=0)
-    return uncond + guide[:, None] * (cond - uncond)
+    return pl.pallas_call(
+        functools.partial(guide_kernel, half=devices // 2),
+        out_shape=jax.ShapeDtypeStruct((pairs_here, width), jnp.float32),
+        in_specs=whole(2, pltpu.VMEM),
+        out_specs=pl.BlockSpec(memory_space=pltpu.HBM),
+        scratch_shapes=[
+            pltpu.VMEM((pairs_here, width), jnp.float32),
+            pltpu.SemaphoreType.DMA(()),
+        ],
+        compiler_params=params,
+        name="guide",
+    )(arrived, guide)
 
 
 def solution(mesh):

time: 44.1 us -> 44 us (level)
  other arithmetic: 0.68 us -> 0 us
  Pallas kernels: 4.62 us -> 5.29 us
    pallas_call x0 -> x1, Pallas kernels: none -> 0.66 us  [on_device(): pl.pallas_call(functools.partial(guide_kernel, half=devices // 2), out_sh...]
    add x1 -> x0, other arithmetic: 0.65 us -> none  [on_device(): return uncond + guide[:, None] * (cond - uncond)]
where the time goes in v5:
time: 44 us; the launch traced here: 43.7 us
  blocking collectives  38.3 us (87%)
  Pallas kernels  5.29 us (12%)
    all_to_all x1, blocking collectives, on_device(): arrived = lax.all_to_all(slots, 'req', 0, 0)  20.3 us
    all_to_all x2, blocking collectives, tp_exchange(): return lax.all_to_all(parts, 'tp', 0, 0)  18.1 us
    pallas_call x1, Pallas kernels, on_device(): pl.pallas_call(attend_kernel, out_shape=parts_shape, in_specs=whole(8, pl...  3.87 us

profile of v5, /device:TPU:2, one launch (start us, length us, event | category | flops | bytes accessed | tf_op | source)
XLA Modules:
  0.0 43.7 jit_solution(2474155229135672166)
XLA Ops:
  0.0 0.0 copy-start
  0.0 0.0 copy-start.1
  0.0 0.0 copy-start.3
  0.0 0.0 copy-start.4
  0.0 0.0 copy-start.2
  0.0 0.0 copy-start.5
  0.0 0.0 copy-start.6
  0.0 3.9 %attend.1 = bf16[8,4,1280]{2,1,0:T(4,128)(2,1)S(1)} custom-call(bf16[4,1280]{1,0:T(4,128)(2,1)} %x_ref.1, f32[1280]{0:T(1024)} %gain_hbm.1, bf16[480,1280]{1,0:T(8,128)(2,1)} %bitcast.1, bf16[4,160,2048]{2,1,0:T(8,128)(2,1)} %k_hbm.1, bf16[4,160,2048]{2,1,0:T(8,128)(2,1)} %v_hbm.1, s32[4]{0:T(128)} %len_hbm.1, s32[4,2048]{1,0:T(4,128)} %pad_hbm.1, ...), custom_call_target="tpu_custom_call" | custom-call | tf_op jit(solution)/shard_map/attend/pallas_call | solution.py:221
  3.9 10.0 %all_to_all.15.parts_ref = bf16[8,4,1280]{2,1,0:T(4,128)(2,1)S(1)} all-to-all(bf16[8,4,1280]{2,1,0:T(4,128)(2,1)S(1)} %attend.1), channel_id=1, replica_groups=mesh['req'=32,'tp'=8] {'tp'}, dimensions={0} | all-to-all | bytes 163840 | tf_op jit(solution)/shard_map/all_to_all | solution.py:195
  13.9 0.0 copy-done
  13.9 0.0 copy-done.1
  13.9 0.0 copy-done.3
  13.9 0.0 copy-done.4
  13.9 0.5 %mlp.1 = (bf16[8,4,1280]{2,1,0:T(4,128)(2,1)S(1)}, f32[4,1280]{1,0:T(4,128)S(1)}) custom-call(bf16[8,4,1280]{2,1,0:T(4,128)(2,1)S(1)} %all_to_all.15.parts_ref, bf16[4,1280]{1,0:T(4,128)(2,1)S(1)} %copy-done.3, f32[1280]{0:T(1024)S(1)} %copy-done.4, bf16[160,1280]{1,0:T(8,128)(2,1)S(1)} %copy-done, bf16[160,1280]{1,0:T(8,128)(2,1)S(1)} %copy-done.1), custom_call_target="tpu_custom_call" | custom-call | tf_op jit(solution)/shard_map/mlp/pallas_call | solution.py:240
  14.4 8.1 %all_to_all.16.parts_ref = bf16[8,4,1280]{2,1,0:T(4,128)(2,1)S(1)} all-to-all(bf16[8,4,1280]{2,1,0:T(4,128)(2,1)S(1)} %get-tuple-element.7), channel_id=1, replica_groups=mesh['req'=32,'tp'=8] {'tp'}, dimensions={0} | all-to-all | bytes 163840 | tf_op jit(solution)/shard_map/all_to_all | solution.py:195
  22.5 0.0 copy-done.2
  22.5 0.0 copy-done.5
  22.5 0.3 head.1
  22.8 20.3 %all_to_all.17.arrived_ref = f32[32,2,160]{2,1,0:T(2,128)S(1)} all-to-all(f32[32,2,160]{2,1,0:T(2,128)S(1)} %head.1), channel_id=1, replica_groups=mesh['req'=32,'tp'=8] {'req'}, dimensions={0} | all-to-all | bytes 81920 | tf_op jit(solution)/shard_map/all_to_all | solution.py:258
  43.0 0.0 copy-done.6
  43.0 0.7 %guide.1 = f32[2,160]{1,0:T(2,128)} custom-call(f32[32,2,160]{2,1,0:T(2,128)S(1)} %all_to_all.17.arrived_ref, f32[2]{0:T(128)S(1)} %copy-done.6), custom_call_target="tpu_custom_call" | custom-call | tf_op jit(solution)/shard_map/guide/pallas_call | solution.py:259
Async XLA Ops:
  0.0 13.9 %copy-start = (bf16[160,1280]{1,0:T(8,128)(2,1)S(1)}, bf16[160,1280]{1,0:T(8,128)(2,1)}, u32[]{:S(2)}) copy-start(bf16[160,1280]{1,0:T(8,128)(2,1)} %up_ref.1) | copy-start | bytes 1228804
  0.0 13.9 %copy-start.1 = (bf16[160,1280]{1,0:T(8,128)(2,1)S(1)}, bf16[160,1280]{1,0:T(8,128)(2,1)}, u32[]{:S(2)}) copy-start(bf16[160,1280]{1,0:T(8,128)(2,1)} %down_ref.1) | copy-start | bytes 1228804
  0.0 13.9 %copy-start.3 = (bf16[4,1280]{1,0:T(4,128)(2,1)S(1)}, bf16[4,1280]{1,0:T(4,128)(2,1)}, u32[]{:S(2)}) copy-start(bf16[4,1280]{1,0:T(4,128)(2,1)} %x_ref.1) | copy-start | bytes 30724
  0.0 13.9 %copy-start.4 = (f32[1280]{0:T(1024)S(1)}, f32[1280]{0:T(1024)}, u32[]{:S(2)}) copy-start(f32[1280]{0:T(1024)} %gain_ref.1) | copy-start | bytes 15364
  0.0 22.5 %copy-start.2 = (bf16[160,1280]{1,0:T(8,128)(2,1)S(1)}, bf16[160,1280]{1,0:T(8,128)(2,1)}, u32[]{:S(2)}) copy-start(bf16[160,1280]{1,0:T(8,128)(2,1)} %head_ref.1) | copy-start | bytes 1228804
  0.0 22.5 %copy-start.5 = (s32[2,64]{1,0:T(2,128)S(1)}, s32[2,64]{1,0:T(2,128)}, u32[]{:S(2)}) copy-start(s32[2,64]{1,0:T(2,128)} %place_ref.1) | copy-start | bytes 1540
  0.0 43.0 %copy-start.6 = (f32[2]{0:T(128)S(1)}, f32[2]{0:T(128)}, u32[]{:S(2)}) copy-start(f32[2]{0:T(128)} %guide_ref.1) | copy-start | bytes 28

commit v6 on v5

--- a/solution.py
+++ b/solution.py
@@ -40,7 +40,13 @@
     len_hbm,
     pad_hbm,
     wo_hbm,
+    up_hbm,
+    down_hbm,
+    head_hbm,
     out_ref,
+    up_ref,
+    down_ref,
+    head_ref,
     x_v,
     gain_v,
     w_v,
@@ -67,6 +73,7 @@
             part = pl.ds(i * group, group)
             copies.append((a.at[part], b.at[part]))
     copies.append((wo_hbm, wo_v))
+    copies += [(up_hbm, up_ref), (down_hbm, down_ref), (head_hbm, head_ref)]
     flights = [pltpu.make_async_copy(a, b, sems.at[i]) for i, (a, b) in enumerate(copies)]
     for flight in flights:
         flight.start()
@@ -74,6 +81,7 @@
     k_in = flights[5 : 5 + BATCHES]
     v_in = flights[5 + BATCHES : 5 + 2 * BATCHES]
     wo_in = flights[5 + 2 * BATCHES]
+    later = flights[6 + 2 * BATCHES :]
     scale = HEAD_DIM ** (-0.5)
 
     owner = lax.broadcasted_iota(jnp.int32, (many, width), 0) // heads
@@ -90,11 +98,13 @@
     valid = valid & (spread(pad_v[...], owner_slot, rows) == 1)
 
     w_in.wait()
-    fused = rows_by_weight(normed, w_v[...]).astype(jnp.bfloat16).astype(jnp.float32)
-    fused = spread(fused, lax.broadcasted_iota(jnp.int32, (many, 3 * width), 0) // heads, rows)
-    query = jnp.where(own_head, fused[:, :width], 0.0)
-    key_new = fused[:, width : 2 * width]
-    value_new = fused[:, 2 * width :]
+    def project(first, count):
+        weight = w_v[pl.ds(first * width, count * width)]
+        flat = rows_by_weight(normed, weight).astype(jnp.bfloat16).astype(jnp.float32)
+        return [spread(flat[:, i * width : (i + 1) * width], owner, rows) for i in range(count)]
+
+    query = jnp.where(own_head, project(0, 1)[0], 0.0)
+    key_new, value_new = project(1, 2)
     own = jnp.sum(query * key_new, axis=1, keepdims=True) * scale
     scores = None
     for r in range(rows):
@@ -105,16 +115,19 @@
         scores = part if scores is None else scores + part
     scores = jnp.where(valid, scores * scale, NEG)
     top = jnp.maximum(jnp.max(scores, axis=1, keepdims=True), own)
-    expo = jnp.where(valid, jnp.exp(scores - top), 0.0)
+    expo = jnp.exp(scores - top)
     own_exp = jnp.exp(own - top)
     inverse = 1.0 / (jnp.sum(expo, axis=1, keepdims=True) + own_exp)
-    probs = (expo * inverse).astype(jnp.bfloat16).astype(jnp.float32)
-    own_prob = (own_exp * inverse).astype(jnp.bfloat16).astype(jnp.float32)
-    fresh = jnp.where(own_head, own_prob * value_new, 0.0)
-    mixed = fresh
-    for h in range(1, heads):
-        mixed = mixed + pltpu.roll(fresh, many - h, 0)
-    mixed = jnp.concatenate([mixed[r * heads : r * heads + 1] for r in range(rows)], axis=0)
+    fresh = jnp.where(own_head, own_exp * inverse * value_new, 0.0)
+    factor = jnp.where(own_head, inverse, 0.0)
+
+    def fold(values):
+        total = values
+        for h in range(1, heads):
+            total = total + pltpu.roll(values, many - h, 0)
+        return jnp.concatenate([total[r * heads : r * heads + 1] for r in range(rows)], axis=0)
+
+    fresh, factor = fold(fresh), fold(factor)
 
     lane = lax.broadcasted_iota(jnp.int32, (width, LANES), 1)
     columns = jnp.zeros((width, LANES), jnp.float32)
@@ -123,7 +136,7 @@
             v_in[r // group].wait()
         sums = []
         for h in range(heads):
-            weights = probs[r * heads + h : r * heads + h + 1]
+            weights = expo[r * heads + h : r * heads + h + 1]
             acc = None
             for c in range(0, slots, LANES):
                 block = v_v[r, pl.ds(h * HEAD_DIM, HEAD_DIM), pl.ds(c, LANES)].astype(jnp.float32)
@@ -132,11 +145,13 @@
             sums.append(acc)
         column = jnp.sum(jnp.concatenate(sums, axis=0), axis=1, keepdims=True)
         columns = jnp.where(lane == r, column, columns)
-    attn = (mixed + columns.T[:rows]).astype(jnp.bfloat16)
+    attn = (fresh + columns.T[:rows] * factor).astype(jnp.bfloat16)
     wo_in.wait()
     terms = jnp.dot(attn, wo_v[...], preferred_element_type=jnp.float32).astype(out_ref.dtype)
     for t in range(out_ref.shape[0]):
         out_ref[t] = terms
+    for flight in later:
+        flight.wait()
 
 
 def mlp_kernel(parts_ref, x_ref, gain_ref, up_ref, down_ref, out_ref, resid_ref):
@@ -218,11 +233,13 @@
     parts_shape = jax.ShapeDtypeStruct((peers, rows, model), jnp.bfloat16)
     fused = w_qkv.reshape(-1, model)
     operands = (inputs, gain_attn, fused, k_cache, v_cache, lengths, pad_mask, w_out)
-    parts = pl.pallas_call(
+    operands += (w_up, w_down, w_head)
+    kept = [jax.ShapeDtypeStruct(w.shape, w.dtype) for w in (w_up, w_down, w_head)]
+    parts, w_up, w_down, w_head = pl.pallas_call(
         attend_kernel,
-        out_shape=parts_shape,
-        in_specs=whole(8, pltpu.HBM),
-        out_specs=pl.BlockSpec(memory_space=pltpu.VMEM),
+        out_shape=(parts_shape, *kept),
+        in_specs=whole(11, pltpu.HBM),
+        out_specs=tuple(whole(4, pltpu.VMEM)),
         scratch_shapes=[
             pltpu.VMEM(inputs.shape, inputs.dtype),
             pltpu.VMEM((model,), jnp.float32),
@@ -232,7 +249,7 @@
             pltpu.SMEM(lengths.shape, lengths.dtype),
             pltpu.VMEM(pad_mask.shape, pad_mask.dtype),
             pltpu.VMEM(w_out.shape, w_out.dtype),
-            pltpu.SemaphoreType.DMA((6 + 2 * BATCHES,)),
+            pltpu.SemaphoreType.DMA((9 + 2 * BATCHES,)),
         ],
         compiler_params=params,
         name="attend",

time: 44 us -> 44 us (level)
  no operation moved by 1% of the time
where the time goes in v6:
time: 44 us; the launch traced here: 43.6 us
  blocking collectives  38.3 us (87%)
  Pallas kernels  5.25 us (12%)
    all_to_all x1, blocking collectives, on_device(): arrived = lax.all_to_all(slots, 'req', 0, 0)  20.3 us
    all_to_all x2, blocking collectives, tp_exchange(): return lax.all_to_all(parts, 'tp', 0, 0)  18.1 us
    pallas_call x1, Pallas kernels, on_device(): pl.pallas_call(attend_kernel, out_shape=(parts_shape, *kept), in_specs=wh...  3.84 us

profile of v6, /device:TPU:2, one launch (start us, length us, event | category | flops | bytes accessed | tf_op | source)
XLA Modules:
  0.0 43.6 jit_solution(6868740401031966049)
XLA Ops:
  0.0 0.0 copy-start
  0.0 0.0 copy-start.1
  0.0 0.0 copy-start.2
  0.0 0.0 copy-start.3
  0.0 3.8 %attend.1 = (bf16[8,4,1280]{2,1,0:T(4,128)(2,1)S(1)}, bf16[160,1280]{1,0:T(8,128)(2,1)S(1)}, bf16[160,1280]{1,0:T(8,128)(2,1)S(1)}, bf16[160,1280]{1,0:T(8,128)(2,1)S(1)}) custom-call(bf16[4,1280]{1,0:T(4,128)(2,1)} %x_ref.1, f32[1280]{0:T(1024)} %gain_hbm.1, bf16[480,1280]{1,0:T(8,128)(2,1)} %bitcast.1, bf16[4,160,2048]{2,1,0:T(8,128)(2,1)} %k_hbm.1, ...), custom_call_target="tpu_custom_call" | custom-call | tf_op jit(solution)/shard_map/attend/pallas_call | solution.py:238
  3.9 10.0 %all_to_all.15.parts_ref = bf16[8,4,1280]{2,1,0:T(4,128)(2,1)S(1)} all-to-all(bf16[8,4,1280]{2,1,0:T(4,128)(2,1)S(1)} %get-tuple-element.11), channel_id=1, replica_groups=mesh['req'=32,'tp'=8] {'tp'}, dimensions={0} | all-to-all | bytes 163840 | tf_op jit(solution)/shard_map/all_to_all | solution.py:210
  13.8 0.0 copy-done
  13.8 0.0 copy-done.1
  13.8 0.5 %mlp.1 = (bf16[8,4,1280]{2,1,0:T(4,128)(2,1)S(1)}, f32[4,1280]{1,0:T(4,128)S(1)}) custom-call(bf16[8,4,1280]{2,1,0:T(4,128)(2,1)S(1)} %all_to_all.15.parts_ref, bf16[4,1280]{1,0:T(4,128)(2,1)S(1)} %copy-done, f32[1280]{0:T(1024)S(1)} %copy-done.1, bf16[160,1280]{1,0:T(8,128)(2,1)S(1)} %get-tuple-element.12.up_ref, ...), custom_call_target="tpu_custom_call" | custom-call | tf_op jit(solution)/shard_map/mlp/pallas_call | solution.py:257
  14.3 8.1 %all_to_all.16.parts_ref = bf16[8,4,1280]{2,1,0:T(4,128)(2,1)S(1)} all-to-all(bf16[8,4,1280]{2,1,0:T(4,128)(2,1)S(1)} %get-tuple-element.14), channel_id=1, replica_groups=mesh['req'=32,'tp'=8] {'tp'}, dimensions={0} | all-to-all | bytes 163840 | tf_op jit(solution)/shard_map/all_to_all | solution.py:210
  22.4 0.0 copy-done.2
  22.4 0.3 head.1
  22.7 20.3 %all_to_all.17.arrived_ref = f32[32,2,160]{2,1,0:T(2,128)S(1)} all-to-all(f32[32,2,160]{2,1,0:T(2,128)S(1)} %head.1), channel_id=1, replica_groups=mesh['req'=32,'tp'=8] {'req'}, dimensions={0} | all-to-all | bytes 81920 | tf_op jit(solution)/shard_map/all_to_all | solution.py:275
  43.0 0.0 copy-done.3
  43.0 0.7 %guide.1 = f32[2,160]{1,0:T(2,128)} custom-call(f32[32,2,160]{2,1,0:T(2,128)S(1)} %all_to_all.17.arrived_ref, f32[2]{0:T(128)S(1)} %copy-done.3), custom_call_target="tpu_custom_call" | custom-call | tf_op jit(solution)/shard_map/guide/pallas_call | solution.py:276
Async XLA Ops:
  0.0 13.8 %copy-start = (bf16[4,1280]{1,0:T(4,128)(2,1)S(1)}, bf16[4,1280]{1,0:T(4,128)(2,1)}, u32[]{:S(2)}) copy-start(bf16[4,1280]{1,0:T(4,128)(2,1)} %x_ref.1) | copy-start | bytes 30724
  0.0 13.8 %copy-start.1 = (f32[1280]{0:T(1024)S(1)}, f32[1280]{0:T(1024)}, u32[]{:S(2)}) copy-start(f32[1280]{0:T(1024)} %gain_ref.1) | copy-start | bytes 15364
  0.0 22.4 %copy-start.2 = (s32[2,64]{1,0:T(2,128)S(1)}, s32[2,64]{1,0:T(2,128)}, u32[]{:S(2)}) copy-start(s32[2,64]{1,0:T(2,128)} %place_ref.1) | copy-start | bytes 1540
  0.0 43.0 %copy-start.3 = (f32[2]{0:T(128)S(1)}, f32[2]{0:T(128)}, u32[]{:S(2)}) copy-start(f32[2]{0:T(128)} %guide_ref.1) | copy-start | bytes 28

commit v7 on v5

--- a/solution.py
+++ b/solution.py
@@ -68,8 +68,8 @@
             copies.append((a.at[part], b.at[part]))
     copies.append((wo_hbm, wo_v))
     flights = [pltpu.make_async_copy(a, b, sems.at[i]) for i, (a, b) in enumerate(copies)]
-    for flight in flights:
-        flight.start()
+    for i, flight in enumerate(flights):
+        flight.start(priority=int(i >= 5 + BATCHES))
     w_in = flights[4]
     k_in = flights[5 : 5 + BATCHES]
     v_in = flights[5 + BATCHES : 5 + 2 * BATCHES]
@@ -90,11 +90,13 @@
     valid = valid & (spread(pad_v[...], owner_slot, rows) == 1)
 
     w_in.wait()
-    fused = rows_by_weight(normed, w_v[...]).astype(jnp.bfloat16).astype(jnp.float32)
-    fused = spread(fused, lax.broadcasted_iota(jnp.int32, (many, 3 * width), 0) // heads, rows)
-    query = jnp.where(own_head, fused[:, :width], 0.0)
-    key_new = fused[:, width : 2 * width]
-    value_new = fused[:, 2 * width :]
+    def project(first, count):
+        weight = w_v[pl.ds(first * width, count * width)]
+        flat = rows_by_weight(normed, weight).astype(jnp.bfloat16).astype(jnp.float32)
+        return [spread(flat[:, i * width : (i + 1) * width], owner, rows) for i in range(count)]
+
+    query = jnp.where(own_head, project(0, 1)[0], 0.0)
+    key_new, value_new = project(1, 2)
     own = jnp.sum(query * key_new, axis=1, keepdims=True) * scale
     scores = None
     for r in range(rows):
@@ -105,7 +107,7 @@
         scores = part if scores is None else scores + part
     scores = jnp.where(valid, scores * scale, NEG)
     top = jnp.maximum(jnp.max(scores, axis=1, keepdims=True), own)
-    expo = jnp.where(valid, jnp.exp(scores - top), 0.0)
+    expo = jnp.exp(scores - top)
     own_exp = jnp.exp(own - top)
     inverse = 1.0 / (jnp.sum(expo, axis=1, keepdims=True) + own_exp)
     probs = (expo * inverse).astype(jnp.bfloat16).astype(jnp.float32)

time: 44 us -> 44 us (level)
  no operation moved by 1% of the time
where the time goes in v7:
time: 44 us; the launch traced here: 43.7 us
  blocking collectives  38.3 us (87%)
  Pallas kernels  5.26 us (12%)
    all_to_all x1, blocking collectives, on_device(): arrived = lax.all_to_all(slots, 'req', 0, 0)  20.3 us
    all_to_all x2, blocking collectives, tp_exchange(): return lax.all_to_all(parts, 'tp', 0, 0)  18.1 us
    pallas_call x1, Pallas kernels, on_device(): pl.pallas_call(attend_kernel, out_shape=parts_shape, in_specs=whole(8, pl...  3.85 us

profile of v7, /device:TPU:2, one launch (start us, length us, event | category | flops | bytes accessed | tf_op | source)
XLA Modules:
  0.0 43.7 jit_solution(1033889420856010738)
XLA Ops:
  0.0 0.0 copy-start
  0.0 0.0 copy-start.1
  0.0 0.0 copy-start.3
  0.0 0.0 copy-start.4
  0.0 0.0 copy-start.2
  0.0 0.0 copy-start.5
  0.0 0.0 copy-start.6
  0.0 3.8 %attend.1 = bf16[8,4,1280]{2,1,0:T(4,128)(2,1)S(1)} custom-call(bf16[4,1280]{1,0:T(4,128)(2,1)} %x_ref.1, f32[1280]{0:T(1024)} %gain_hbm.1, bf16[480,1280]{1,0:T(8,128)(2,1)} %bitcast.1, bf16[4,160,2048]{2,1,0:T(8,128)(2,1)} %k_hbm.1, bf16[4,160,2048]{2,1,0:T(8,128)(2,1)} %v_hbm.1, s32[4]{0:T(128)} %len_hbm.1, s32[4,2048]{1,0:T(4,128)} %pad_hbm.1, ...), custom_call_target="tpu_custom_call" | custom-call | tf_op jit(solution)/shard_map/attend/pallas_call | solution.py:223
  3.9 10.0 %all_to_all.15.parts_ref = bf16[8,4,1280]{2,1,0:T(4,128)(2,1)S(1)} all-to-all(bf16[8,4,1280]{2,1,0:T(4,128)(2,1)S(1)} %attend.1), channel_id=1, replica_groups=mesh['req'=32,'tp'=8] {'tp'}, dimensions={0} | all-to-all | bytes 163840 | tf_op jit(solution)/shard_map/all_to_all | solution.py:197
  13.9 0.0 copy-done
  13.9 0.0 copy-done.1
  13.9 0.0 copy-done.3
  13.9 0.0 copy-done.4
  13.9 0.5 %mlp.1 = (bf16[8,4,1280]{2,1,0:T(4,128)(2,1)S(1)}, f32[4,1280]{1,0:T(4,128)S(1)}) custom-call(bf16[8,4,1280]{2,1,0:T(4,128)(2,1)S(1)} %all_to_all.15.parts_ref, bf16[4,1280]{1,0:T(4,128)(2,1)S(1)} %copy-done.3, f32[1280]{0:T(1024)S(1)} %copy-done.4, bf16[160,1280]{1,0:T(8,128)(2,1)S(1)} %copy-done, bf16[160,1280]{1,0:T(8,128)(2,1)S(1)} %copy-done.1), custom_call_target="tpu_custom_call" | custom-call | tf_op jit(solution)/shard_map/mlp/pallas_call | solution.py:242
  14.4 8.1 %all_to_all.16.parts_ref = bf16[8,4,1280]{2,1,0:T(4,128)(2,1)S(1)} all-to-all(bf16[8,4,1280]{2,1,0:T(4,128)(2,1)S(1)} %get-tuple-element.7), channel_id=1, replica_groups=mesh['req'=32,'tp'=8] {'tp'}, dimensions={0} | all-to-all | bytes 163840 | tf_op jit(solution)/shard_map/all_to_all | solution.py:197
  22.5 0.0 copy-done.2
  22.5 0.0 copy-done.5
  22.5 0.3 head.1
  22.8 20.3 %all_to_all.17.arrived_ref = f32[32,2,160]{2,1,0:T(2,128)S(1)} all-to-all(f32[32,2,160]{2,1,0:T(2,128)S(1)} %head.1), channel_id=1, replica_groups=mesh['req'=32,'tp'=8] {'req'}, dimensions={0} | all-to-all | bytes 81920 | tf_op jit(solution)/shard_map/all_to_all | solution.py:260
  43.0 0.0 copy-done.6
  43.0 0.7 %guide.1 = f32[2,160]{1,0:T(2,128)} custom-call(f32[32,2,160]{2,1,0:T(2,128)S(1)} %all_to_all.17.arrived_ref, f32[2]{0:T(128)S(1)} %copy-done.6), custom_call_target="tpu_custom_call" | custom-call | tf_op jit(solution)/shard_map/guide/pallas_call | solution.py:261
Async XLA Ops:
  0.0 13.9 %copy-start = (bf16[160,1280]{1,0:T(8,128)(2,1)S(1)}, bf16[160,1280]{1,0:T(8,128)(2,1)}, u32[]{:S(2)}) copy-start(bf16[160,1280]{1,0:T(8,128)(2,1)} %up_ref.1) | copy-start | bytes 1228804
  0.0 13.9 %copy-start.1 = (bf16[160,1280]{1,0:T(8,128)(2,1)S(1)}, bf16[160,1280]{1,0:T(8,128)(2,1)}, u32[]{:S(2)}) copy-start(bf16[160,1280]{1,0:T(8,128)(2,1)} %down_ref.1) | copy-start | bytes 1228804
  0.0 13.9 %copy-start.3 = (bf16[4,1280]{1,0:T(4,128)(2,1)S(1)}, bf16[4,1280]{1,0:T(4,128)(2,1)}, u32[]{:S(2)}) copy-start(bf16[4,1280]{1,0:T(4,128)(2,1)} %x_ref.1) | copy-start | bytes 30724
  0.0 13.9 %copy-start.4 = (f32[1280]{0:T(1024)S(1)}, f32[1280]{0:T(1024)}, u32[]{:S(2)}) copy-start(f32[1280]{0:T(1024)} %gain_ref.1) | copy-start | bytes 15364
  0.0 22.5 %copy-start.2 = (bf16[160,1280]{1,0:T(8,128)(2,1)S(1)}, bf16[160,1280]{1,0:T(8,128)(2,1)}, u32[]{:S(2)}) copy-start(bf16[160,1280]{1,0:T(8,128)(2,1)} %head_ref.1) | copy-start | bytes 1228804
  0.0 22.5 %copy-start.5 = (s32[2,64]{1,0:T(2,128)S(1)}, s32[2,64]{1,0:T(2,128)}, u32[]{:S(2)}) copy-start(s32[2,64]{1,0:T(2,128)} %place_ref.1) | copy-start | bytes 1540
  0.0 43.0 %copy-start.6 = (f32[2]{0:T(128)S(1)}, f32[2]{0:T(128)}, u32[]{:S(2)}) copy-start(f32[2]{0:T(128)} %guide_ref.1) | copy-start | bytes 28
